TPU v7x, 512 devices: a whole 4x4x16 slice. The times are simulated.
512 devices in a mesh: fsdp: 16 (over z), replica: 16 (over x_lo, y, core), tm: 2 (over x_hi).
Axes of the slice: x: 4 (x_hi: 2, x_lo: 2; x = x_hi * 2 + x_lo), y: 4, z: 16, core: 2. Of those that a mesh axis runs over, the one named last changes fastest.
Arguments:
- clip_input: bfloat16 [16, 8, 16, 16, 512], P('replica', 'tm'), may hold values from -6 to 6
- first_kernel: bfloat16 [27, 512, 512], P(None, None, 'fsdp'), may hold values from -0.0546875 to 0.0546875
- second_kernel: bfloat16 [27, 512, 512], P(None, 'fsdp'), may hold values from -0.0546875 to 0.0546875
- out_grad: bfloat16 [16, 2, 4, 4, 512], P('replica', 'tm'), may hold values from -1 to 1
- tap_mix: float32 [2, 27, 27], replicated, may hold values from -0.14 to 1.4
- left_panels: float32 [2, 512, 512], P(None, 'fsdp'), may hold values from -0.05 to 2
- right_panels: float32 [2, 512, 512], P(None, 'fsdp', ('replica', 'tm')), may hold values from -0.05 to 2
Outputs:
- update: bfloat16 [2, 27, 512, 512], P(None, None, 'fsdp', ('replica', 'tm'))
All inputs are finite; a program needn't handle non-finite values.
Results may differ from a plain program's by a relative error of at most 0.0049.
Values may be sent and summed in bfloat16 or wider, within the bound.
A program may use at most 128 MiB of HBM per device.

v0:
```python
import jax
import jax.numpy as jnp
from jax import lax
from jax.sharding import PartitionSpec as P

TAPS = 27


def shifted(block, axis, distance):
    devices = range(lax.axis_size(axis))
    route = [(i - distance, i) for i in devices if i - distance in devices]
    return lax.ppermute(block, axis, route)


def tap_patches(padded, out_frames, out_side):
    pieces_list = []
    for tap_index in range(TAPS):
        along_time = tap_index // 9
        along_rows = tap_index // 3 % 3
        along_cols = tap_index % 3
        pieces_list.append(
            padded[
                :,
                along_time : along_time + 2 * out_frames : 2,
                along_rows : along_rows + 2 * out_side : 2,
                along_cols : along_cols + 2 * out_side : 2,
                :,
            ]
        )
    return jnp.concatenate(pieces_list, axis=-1)


def spread_back(grad_shape, columns, out_frames, out_side, channels):
    total = jnp.zeros(grad_shape, jnp.float32)
    for tap_index in range(TAPS):
        along_time = tap_index // 9
        along_rows = tap_index // 3 % 3
        along_cols = tap_index % 3
        total = total.at[
            :,
            along_time : along_time + 2 * out_frames : 2,
            along_rows : along_rows + 2 * out_side : 2,
            along_cols : along_cols + 2 * out_side : 2,
            :,
        ].add(columns[..., tap_index * channels : (tap_index + 1) * channels])
    return total


def shards(clip_input, first_kernel, second_kernel, out_grad, tap_mix, left_panels, right_panels):
    highest = lax.Precision.HIGHEST
    clip_count = clip_input.shape[0]
    frames = clip_input.shape[1]
    side_cells = clip_input.shape[2]
    channels = clip_input.shape[4]
    own_width = first_kernel.shape[2]
    half_frames = frames // 2
    half_side = side_cells // 2
    quarter_frames = frames // 4
    quarter_side = side_cells // 4
    spatial_pad = ((0, 0), (0, 0), (1, 0), (1, 0), (0, 0))
    flat_kernel = first_kernel.reshape(TAPS * channels, own_width)
    prior_frame = shifted(clip_input[:, frames - 1 :], "tm", 1)
    extended = jnp.concatenate([prior_frame, clip_input], axis=1)
    padded_input = jnp.pad(extended, spatial_pad)
    first_patches = tap_patches(padded_input, half_frames, half_side).reshape(-1, TAPS * channels)
    pre_act = jnp.dot(first_patches, flat_kernel, preferred_element_type=jnp.float32)
    hidden = (
        jax.nn.silu(pre_act)
        .astype(jnp.bfloat16)
        .reshape(clip_count, half_frames, half_side, half_side, own_width)
    )
    prior_hidden = shifted(hidden[:, half_frames - 1 :], "tm", 1)
    padded_hidden = jnp.pad(jnp.concatenate([prior_hidden, hidden], axis=1), spatial_pad)
    second_patches = tap_patches(padded_hidden, quarter_frames, quarter_side).reshape(
        -1, TAPS * own_width
    )
    grad_rows = out_grad.reshape(-1, channels)
    second_grad = jnp.dot(grad_rows.T, second_patches, preferred_element_type=jnp.float32)
    second_grad = second_grad.reshape(channels, TAPS, own_width).transpose(1, 0, 2)
    back_columns = jnp.dot(
        grad_rows,
        second_kernel.reshape(TAPS * own_width, channels).T,
        preferred_element_type=jnp.float32,
    )
    back_columns = back_columns.reshape(
        clip_count, quarter_frames, quarter_side, quarter_side, TAPS * own_width
    )
    spread = spread_back(padded_hidden.shape, back_columns, quarter_frames, quarter_side, own_width)
    returned = shifted(spread[:, :1, 1:, 1:, :], "tm", -1)
    hidden_grad = spread[:, 1:, 1:, 1:, :]
    hidden_grad = hidden_grad.at[:, half_frames - 1 :].add(returned).reshape(-1, own_width)
    sigmoid_vals = jax.nn.sigmoid(pre_act)
    pre_grad = (hidden_grad * sigmoid_vals * (1.0 + pre_act * (1.0 - sigmoid_vals))).astype(
        jnp.bfloat16
    )
    first_grad = jnp.dot(first_patches.T, pre_grad, preferred_element_type=jnp.float32).reshape(
        TAPS, channels, own_width
    )
    stacked = jnp.stack([first_grad, second_grad])
    summed = lax.psum(stacked, ("replica", "tm"))
    tap_mixed = jnp.einsum("lst,ltij->lsij", tap_mix, summed, precision=highest)
    left_done = jnp.einsum(
        "lik,lskj->lsij",
        lax.all_gather(left_panels, "fsdp", axis=1, tiled=True),
        tap_mixed,
        precision=highest,
    )
    result = lax.psum_scatter(
        jnp.einsum("lsij,ljk->ilsk", left_done, right_panels, precision=highest),
        "fsdp",
        scatter_dimension=0,
        tiled=True,
    ).transpose(1, 2, 0, 3)
    return result.astype(jnp.bfloat16)


def solution(mesh):
    in_specs = (
        P("replica", "tm", None, None, None),
        P(None, None, "fsdp"),
        P(None, "fsdp", None),
        P("replica", "tm", None, None, None),
        P(),
        P(None, "fsdp", None),
        P(None, "fsdp", ("replica", "tm")),
    )
    out_specs = P(None, None, "fsdp", ("replica", "tm"))
    return jax.shard_map(shards, mesh=mesh, in_specs=in_specs, out_specs=out_specs, check_vma=False)
```

profile of v0, /device:TPU:6, one launch (start us, length us, event | category | flops | bytes accessed | tf_op | source)
XLA Modules:
  0.0 490.0 jit_solution(18250001880252223688)
XLA Ops:
  14.3 1.5 scatter_fusion
  15.8 1.5 scatter_fusion.1
  17.3 1.5 scatter_fusion.2
  18.8 1.5 scatter_fusion.3
  20.3 1.5 scatter_fusion.4
  21.8 1.5 scatter_fusion.5
  23.3 1.5 scatter_fusion.6
  24.8 1.5 scatter_fusion.7
  32.2 2.0 scatter_fusion.12
  34.3 1.5 scatter_fusion.13
  47.7 1.5 scatter_fusion.22
  50.7 1.7 scatter_fusion.24
  52.3 1.5 scatter_fusion.25
  55.4 6.1 %collective-permute-start.1 = (f32[1,1,8,8,32]{4,1,3,2,0:T(1,128)S(1)}, f32[1,1,8,8,32]{4,1,3,2,0:T(1,128)S(1)}, u32[]{:S(2)}, u32[]{:S(2)}) collective-permute-start(f32[1,1,8,8,32]{4,1,3,2,0:T(1,128)S(1)} %slice.702), channel_id=1, source_target_pairs={{1,0},{3,2},{5,4},{7,6},{9,8},{11,10},{13,12},{15,14},{17,16},{19,... | collective-permute-start | bytes 24584 | tf_op jit(solution)/shard_map/ppermute | solution.py:12
  63.3 2.2 fusion.15
  65.5 5.0 %slice.318 = bf16[1,2,8,8,512]{4,3,2,1,0:T(8,128)(2,1)} slice(bf16[1,5,17,17,512]{4,3,2,1,0:T(8,128)(2,1)S(1)} %fusion.15), slice={[0:1:1], [0:4:2], [0:16:2], [0:16:2], [0:512:1]} | slice | bytes 262144 | tf_op jit(solution)/shard_map/slice | solution.py:22
  70.5 4.9 %slice.319 = bf16[1,2,8,8,512]{4,3,2,1,0:T(8,128)(2,1)} slice(bf16[1,5,17,17,512]{4,3,2,1,0:T(8,128)(2,1)S(1)} %fusion.15), slice={[0:1:1], [0:4:2], [0:16:2], [1:17:2], [0:512:1]} | slice | bytes 262144 | tf_op jit(solution)/shard_map/slice | solution.py:22
  75.4 5.0 %slice.320 = bf16[1,2,8,8,512]{4,3,2,1,0:T(8,128)(2,1)} slice(bf16[1,5,17,17,512]{4,3,2,1,0:T(8,128)(2,1)S(1)} %fusion.15), slice={[0:1:1], [0:4:2], [0:16:2], [2:17:2], [0:512:1]} | slice | bytes 262144 | tf_op jit(solution)/shard_map/slice | solution.py:22
  80.4 4.9 %slice.321 = bf16[1,2,8,8,512]{4,3,2,1,0:T(8,128)(2,1)} slice(bf16[1,5,17,17,512]{4,3,2,1,0:T(8,128)(2,1)S(1)} %fusion.15), slice={[0:1:1], [0:4:2], [1:17:2], [0:16:2], [0:512:1]} | slice | bytes 262144 | tf_op jit(solution)/shard_map/slice | solution.py:22
  85.3 4.9 %slice.322 = bf16[1,2,8,8,512]{4,3,2,1,0:T(8,128)(2,1)} slice(bf16[1,5,17,17,512]{4,3,2,1,0:T(8,128)(2,1)S(1)} %fusion.15), slice={[0:1:1], [0:4:2], [1:17:2], [1:17:2], [0:512:1]} | slice | bytes 262144 | tf_op jit(solution)/shard_map/slice | solution.py:22
  90.2 5.0 %slice.323 = bf16[1,2,8,8,512]{4,3,2,1,0:T(8,128)(2,1)} slice(bf16[1,5,17,17,512]{4,3,2,1,0:T(8,128)(2,1)S(1)} %fusion.15), slice={[0:1:1], [0:4:2], [1:17:2], [2:17:2], [0:512:1]} | slice | bytes 262144 | tf_op jit(solution)/shard_map/slice | solution.py:22
  95.2 5.0 %slice.324 = bf16[1,2,8,8,512]{4,3,2,1,0:T(8,128)(2,1)} slice(bf16[1,5,17,17,512]{4,3,2,1,0:T(8,128)(2,1)S(1)} %fusion.15), slice={[0:1:1], [0:4:2], [2:17:2], [0:16:2], [0:512:1]} | slice | bytes 262144 | tf_op jit(solution)/shard_map/slice | solution.py:22
  100.2 4.9 %slice.325 = bf16[1,2,8,8,512]{4,3,2,1,0:T(8,128)(2,1)} slice(bf16[1,5,17,17,512]{4,3,2,1,0:T(8,128)(2,1)S(1)} %fusion.15), slice={[0:1:1], [0:4:2], [2:17:2], [1:17:2], [0:512:1]} | slice | bytes 262144 | tf_op jit(solution)/shard_map/slice | solution.py:22
  105.1 5.0 %slice.326 = bf16[1,2,8,8,512]{4,3,2,1,0:T(8,128)(2,1)} slice(bf16[1,5,17,17,512]{4,3,2,1,0:T(8,128)(2,1)S(1)} %fusion.15), slice={[0:1:1], [0:4:2], [2:17:2], [2:17:2], [0:512:1]} | slice | bytes 262144 | tf_op jit(solution)/shard_map/slice | solution.py:22
  110.1 4.9 %slice.327 = bf16[1,2,8,8,512]{4,3,2,1,0:T(8,128)(2,1)} slice(bf16[1,5,17,17,512]{4,3,2,1,0:T(8,128)(2,1)S(1)} %fusion.15), slice={[0:1:1], [1:5:2], [0:16:2], [0:16:2], [0:512:1]} | slice | bytes 262144 | tf_op jit(solution)/shard_map/slice | solution.py:22
  115.0 4.9 %slice.328 = bf16[1,2,8,8,512]{4,3,2,1,0:T(8,128)(2,1)} slice(bf16[1,5,17,17,512]{4,3,2,1,0:T(8,128)(2,1)S(1)} %fusion.15), slice={[0:1:1], [1:5:2], [0:16:2], [1:17:2], [0:512:1]} | slice | bytes 262144 | tf_op jit(solution)/shard_map/slice | solution.py:22
  119.9 5.0 %slice.329 = bf16[1,2,8,8,512]{4,3,2,1,0:T(8,128)(2,1)} slice(bf16[1,5,17,17,512]{4,3,2,1,0:T(8,128)(2,1)S(1)} %fusion.15), slice={[0:1:1], [1:5:2], [0:16:2], [2:17:2], [0:512:1]} | slice | bytes 262144 | tf_op jit(solution)/shard_map/slice | solution.py:22
  124.9 4.9 %slice.330 = bf16[1,2,8,8,512]{4,3,2,1,0:T(8,128)(2,1)} slice(bf16[1,5,17,17,512]{4,3,2,1,0:T(8,128)(2,1)S(1)} %fusion.15), slice={[0:1:1], [1:5:2], [1:17:2], [0:16:2], [0:512:1]} | slice | bytes 262144 | tf_op jit(solution)/shard_map/slice | solution.py:22
  129.8 4.9 %slice.331 = bf16[1,2,8,8,512]{4,3,2,1,0:T(8,128)(2,1)} slice(bf16[1,5,17,17,512]{4,3,2,1,0:T(8,128)(2,1)S(1)} %fusion.15), slice={[0:1:1], [1:5:2], [1:17:2], [1:17:2], [0:512:1]} | slice | bytes 262144 | tf_op jit(solution)/shard_map/slice | solution.py:22
  134.7 5.0 %slice.332 = bf16[1,2,8,8,512]{4,3,2,1,0:T(8,128)(2,1)} slice(bf16[1,5,17,17,512]{4,3,2,1,0:T(8,128)(2,1)S(1)} %fusion.15), slice={[0:1:1], [1:5:2], [1:17:2], [2:17:2], [0:512:1]} | slice | bytes 262144 | tf_op jit(solution)/shard_map/slice | solution.py:22
  139.7 4.9 %slice.333 = bf16[1,2,8,8,512]{4,3,2,1,0:T(8,128)(2,1)} slice(bf16[1,5,17,17,512]{4,3,2,1,0:T(8,128)(2,1)S(1)} %fusion.15), slice={[0:1:1], [1:5:2], [2:17:2], [0:16:2], [0:512:1]} | slice | bytes 262144 | tf_op jit(solution)/shard_map/slice | solution.py:22
  144.6 4.9 %slice.334 = bf16[1,2,8,8,512]{4,3,2,1,0:T(8,128)(2,1)} slice(bf16[1,5,17,17,512]{4,3,2,1,0:T(8,128)(2,1)S(1)} %fusion.15), slice={[0:1:1], [1:5:2], [2:17:2], [1:17:2], [0:512:1]} | slice | bytes 262144 | tf_op jit(solution)/shard_map/slice | solution.py:22
  149.6 5.0 %slice.335 = bf16[1,2,8,8,512]{4,3,2,1,0:T(8,128)(2,1)} slice(bf16[1,5,17,17,512]{4,3,2,1,0:T(8,128)(2,1)S(1)} %fusion.15), slice={[0:1:1], [1:5:2], [2:17:2], [2:17:2], [0:512:1]} | slice | bytes 262144 | tf_op jit(solution)/shard_map/slice | solution.py:22
  154.6 4.9 %slice.336 = bf16[1,2,8,8,512]{4,3,2,1,0:T(8,128)(2,1)} slice(bf16[1,5,17,17,512]{4,3,2,1,0:T(8,128)(2,1)S(1)} %fusion.15), slice={[0:1:1], [2:5:2], [0:16:2], [0:16:2], [0:512:1]} | slice | bytes 262144 | tf_op jit(solution)/shard_map/slice | solution.py:22
  159.5 4.9 %slice.337 = bf16[1,2,8,8,512]{4,3,2,1,0:T(8,128)(2,1)} slice(bf16[1,5,17,17,512]{4,3,2,1,0:T(8,128)(2,1)S(1)} %fusion.15), slice={[0:1:1], [2:5:2], [0:16:2], [1:17:2], [0:512:1]} | slice | bytes 262144 | tf_op jit(solution)/shard_map/slice | solution.py:22
  164.4 5.0 %slice.338 = bf16[1,2,8,8,512]{4,3,2,1,0:T(8,128)(2,1)} slice(bf16[1,5,17,17,512]{4,3,2,1,0:T(8,128)(2,1)S(1)} %fusion.15), slice={[0:1:1], [2:5:2], [0:16:2], [2:17:2], [0:512:1]} | slice | bytes 262144 | tf_op jit(solution)/shard_map/slice | solution.py:22
  169.4 4.9 %slice.339 = bf16[1,2,8,8,512]{4,3,2,1,0:T(8,128)(2,1)} slice(bf16[1,5,17,17,512]{4,3,2,1,0:T(8,128)(2,1)S(1)} %fusion.15), slice={[0:1:1], [2:5:2], [1:17:2], [0:16:2], [0:512:1]} | slice | bytes 262144 | tf_op jit(solution)/shard_map/slice | solution.py:22
  174.3 4.9 %slice.340 = bf16[1,2,8,8,512]{4,3,2,1,0:T(8,128)(2,1)} slice(bf16[1,5,17,17,512]{4,3,2,1,0:T(8,128)(2,1)S(1)} %fusion.15), slice={[0:1:1], [2:5:2], [1:17:2], [1:17:2], [0:512:1]} | slice | bytes 262144 | tf_op jit(solution)/shard_map/slice | solution.py:22
  182.0 1.7 constant_dynamic-update-slice_fusion.26
  183.8 1.6 constant_dynamic-update-slice_fusion.25
  185.4 1.6 constant_dynamic-update-slice_fusion.24
  186.9 1.6 constant_dynamic-update-slice_fusion.23
  188.5 1.6 constant_dynamic-update-slice_fusion.22
  190.1 1.6 constant_dynamic-update-slice_fusion.21
  191.7 1.6 constant_dynamic-update-slice_fusion.20
  193.3 1.6 constant_dynamic-update-slice_fusion.19
  194.9 1.6 constant_dynamic-update-slice_fusion.18
  196.5 1.6 constant_dynamic-update-slice_fusion.17
  198.0 1.6 constant_dynamic-update-slice_fusion.16
  199.6 1.6 constant_dynamic-update-slice_fusion.15
  201.2 1.6 constant_dynamic-update-slice_fusion.14
  202.8 1.6 constant_dynamic-update-slice_fusion.13
  213.2 6.0 %copy.17 = bf16[128,13824]{0,1:T(8,128)(2,1)} copy(bf16[128,13824]{1,0:T(8,128)(2,1)} %bitcast) | data formatting | bytes 7077888 | tf_op jit(solution)/shard_map/reshape | solution.py:65
  219.2 3.2 multiply_convert_fusion
  223.9 3.3 convolution_bitcast_fusion
  227.2 2.5 collective-permute-done.2
  234.4 2.2 pad_maximum_fusion
  237.5 146.2 %all-reduce.4.cloned.1.call-done = f32[2,27,512,32]{2,3,1,0:T(8,128)} async-done(((f32[2,27,512,32]{2,3,1,0:T(8,128)}), f32[2,27,512,32]{2,3,1,0:T(8,128)}) %all-reduce.4.cloned.1.call-update) | async-done | bytes 3538960 | tf_op jit(solution)/shard_map/psum | solution.py:100
  383.7 10.7 %fusion.11 = f32[2,27,512,32]{2,1,3,0:T(8,128)} fusion(f32[2,27,512,32]{2,3,1,0:T(8,128)} %all-reduce.4.cloned.1.call-done, f32[2,27,27,1]{2,0,1,3:T(2,128)S(1)} %bitcast.215), kind=kOutput, calls=%fused_computation.41 | convolution fusion | flops 286654464 | bytes 7083720 | tf_op jit(solution)/shard_map/lst,ltij->lsij/dot_general | solution.py:101
  394.4 10.1 %fusion.7 = f32[2,27,32,512]{3,2,1,0:T(8,128)S(1)} fusion(f32[2,27,512,32]{2,1,3,0:T(8,128)} %fusion.11, f32[2,512,512]{2,1,0:T(8,128)} %all-gather.2.cloned.1.call-done), kind=kOutput, calls=%fused_computation.37 | convolution fusion | flops 5435817984 | bytes 9175040 | tf_op jit(solution)/shard_map/lik,lskj->lsij/dot_general | solution.py:102
  404.5 2.0 fusion.5
  406.6 1.7 copy.32
  408.3 72.3 %reduce-scatter.4.cloned.1.call-done = f32[32,864]{1,0:T(8,128)} async-done(((f32[512,864]{1,0:T(8,128)}), f32[32,864]{1,0:T(8,128)}) %reduce-scatter.4.cloned.1.call-update) | async-done | bytes 110608
  480.6 1.7 copy.33
  (174 shorter events, 47.7 us)
Async XLA Ops:
  7.4 3.1 copy-start
  7.4 54.1 %copy-start.2 = (bf16[27,512,32]{1,2,0:T(8,128)(2,1)S(1)}, bf16[27,512,32]{1,2,0:T(8,128)(2,1)}, u32[]{:S(2)}) copy-start(bf16[27,512,32]{1,2,0:T(8,128)(2,1)} %param.10) | copy-start | bytes 2654212
  7.4 376.3 %all-reduce.4.cloned.1.call-start = ((), (), s32[]{:S(2)}) async-start(), calls=%async_computation.1 | async-start | bytes 7077888 | tf_op jit(solution)/shard_map/psum | solution.py:100
  8.5 54.8 %collective-permute-start = (bf16[1,1,16,16,512]{4,3,2,1,0:T(8,128)(2,1)S(1)}, bf16[1,1,16,16,512]{4,3,2,1,0:T(8,128)(2,1)S(1)}, u32[]{:S(2)}, u32[]{:S(2)}) collective-permute-start(bf16[1,1,16,16,512]{4,3,2,1,0:T(8,128)(2,1)S(1)} %slice.317), channel_id=1, source_target_pairs={{0,1},{2,3},{4,5},{6,7},{8,9},{10,11},{12,13},{14,15},{16,17},{18,... | collective-permute-start | bytes 786440 | tf_op jit(solution)/shard_map/ppermute | solution.py:12
  55.4 7.7 %collective-permute-start.1 = (f32[1,1,8,8,32]{4,1,3,2,0:T(1,128)S(1)}, f32[1,1,8,8,32]{4,1,3,2,0:T(1,128)S(1)}, u32[]{:S(2)}, u32[]{:S(2)}) collective-permute-start(f32[1,1,8,8,32]{4,1,3,2,0:T(1,128)S(1)} %slice.702), channel_id=1, source_target_pairs={{1,0},{3,2},{5,4},{7,6},{9,8},{11,10},{13,12},{15,14},{17,16},{19,... | collective-permute-start | bytes 24584 | tf_op jit(solution)/shard_map/ppermute | solution.py:12
  182.0 22.4 %copy-start.11 = (bf16[1,2,8,8,512]{4,3,2,1,0:T(8,128)(2,1)S(1)}, bf16[1,2,8,8,512]{4,3,2,1,0:T(8,128)(2,1)}, u32[]{:S(2)}) copy-start(bf16[1,2,8,8,512]{4,3,2,1,0:T(8,128)(2,1)} %slice.332) | copy-start | bytes 393220
  182.0 23.1 %copy-start.10 = (bf16[1,2,8,8,512]{4,3,2,1,0:T(8,128)(2,1)S(1)}, bf16[1,2,8,8,512]{4,3,2,1,0:T(8,128)(2,1)}, u32[]{:S(2)}) copy-start(bf16[1,2,8,8,512]{4,3,2,1,0:T(8,128)(2,1)} %slice.333) | copy-start | bytes 393220
  182.0 23.7 %copy-start.9 = (bf16[1,2,8,8,512]{4,3,2,1,0:T(8,128)(2,1)S(1)}, bf16[1,2,8,8,512]{4,3,2,1,0:T(8,128)(2,1)}, u32[]{:S(2)}) copy-start(bf16[1,2,8,8,512]{4,3,2,1,0:T(8,128)(2,1)} %slice.334) | copy-start | bytes 393220
  182.0 24.4 %copy-start.8 = (bf16[1,2,8,8,512]{4,3,2,1,0:T(8,128)(2,1)S(1)}, bf16[1,2,8,8,512]{4,3,2,1,0:T(8,128)(2,1)}, u32[]{:S(2)}) copy-start(bf16[1,2,8,8,512]{4,3,2,1,0:T(8,128)(2,1)} %slice.335) | copy-start | bytes 393220
  182.0 25.1 %copy-start.7 = (bf16[1,2,8,8,512]{4,3,2,1,0:T(8,128)(2,1)S(1)}, bf16[1,2,8,8,512]{4,3,2,1,0:T(8,128)(2,1)}, u32[]{:S(2)}) copy-start(bf16[1,2,8,8,512]{4,3,2,1,0:T(8,128)(2,1)} %slice.336) | copy-start | bytes 393220
  182.0 25.8 %copy-start.6 = (bf16[1,2,8,8,512]{4,3,2,1,0:T(8,128)(2,1)S(1)}, bf16[1,2,8,8,512]{4,3,2,1,0:T(8,128)(2,1)}, u32[]{:S(2)}) copy-start(bf16[1,2,8,8,512]{4,3,2,1,0:T(8,128)(2,1)} %slice.337) | copy-start | bytes 393220
  182.0 26.4 %copy-start.5 = (bf16[1,2,8,8,512]{4,3,2,1,0:T(8,128)(2,1)S(1)}, bf16[1,2,8,8,512]{4,3,2,1,0:T(8,128)(2,1)}, u32[]{:S(2)}) copy-start(bf16[1,2,8,8,512]{4,3,2,1,0:T(8,128)(2,1)} %slice.338) | copy-start | bytes 393220
  182.0 27.1 %copy-start.4 = (bf16[1,2,8,8,512]{4,3,2,1,0:T(8,128)(2,1)S(1)}, bf16[1,2,8,8,512]{4,3,2,1,0:T(8,128)(2,1)}, u32[]{:S(2)}) copy-start(bf16[1,2,8,8,512]{4,3,2,1,0:T(8,128)(2,1)} %slice.339) | copy-start | bytes 393220
  182.0 27.7 %copy-start.3 = (bf16[1,2,8,8,512]{4,3,2,1,0:T(8,128)(2,1)S(1)}, bf16[1,2,8,8,512]{4,3,2,1,0:T(8,128)(2,1)}, u32[]{:S(2)}) copy-start(bf16[1,2,8,8,512]{4,3,2,1,0:T(8,128)(2,1)} %slice.340) | copy-start | bytes 393220
  213.2 6.0 %copy-start.1 = (bf16[27,4,8,512]{3,2,0,1:T(8,128)(2,1)S(1)}, bf16[27,4,8,512]{3,2,0,1:T(8,128)(2,1)}, u32[]{:S(2)}) copy-start(bf16[27,4,8,512]{3,2,0,1:T(8,128)(2,1)} %copy.34) | copy-start | bytes 2654212
  222.4 11.5 %copy-start.14 = (bf16[1,1,4,4,512]{4,3,2,1,0:T(4,128)(2,1)S(1)}, bf16[1,1,4,4,512]{4,3,2,1,0:T(4,128)(2,1)}, u32[]{:S(2)}) copy-start(bf16[1,1,4,4,512]{4,3,2,1,0:T(4,128)(2,1)} %param.12) | copy-start | bytes 49156
  222.6 7.1 %collective-permute-start.2 = (bf16[1,1,8,8,32]{4,3,2,1,0:T(8,128)(2,1)S(1)}, bf16[1,1,8,8,32]{4,3,2,1,0:T(8,128)(2,1)S(1)}, u32[]{:S(2)}, u32[]{:S(2)}) collective-permute-start(bf16[1,1,8,8,32]{4,3,2,1,0:T(8,128)(2,1)S(1)} %slice.703), channel_id=1, source_target_pairs={{0,1},{2,3},{4,5},{6,7},{8,9},{10,11},{12,13},{14,15},{16,17},{18,... | collective-permute-start | bytes 12296 | tf_op jit(solution)/shard_map/ppermute | solution.py:12
  236.6 147.1 %copy-start.12 = (f32[2,27,27]{2,0,1:T(2,128)S(1)}, f32[2,27,27]{2,0,1:T(2,128)}, u32[]{:S(2)}) copy-start(f32[2,27,27]{2,0,1:T(2,128)} %param.13) | copy-start | bytes 17500
  236.6 157.8 %all-gather.2.cloned.1.call-start = ((), (), s32[]{:S(2)}) async-start(), calls=%async_computation.2 | async-start | bytes 2228224 | tf_op jit(solution)/shard_map/all_gather | solution.py:104
  237.2 243.4 %reduce-scatter.4.cloned.1.call-start = ((), (), s32[]{:S(2)}) async-start(), calls=%async_computation.3 | async-start | bytes 1949696
  394.4 10.1 %copy-start.13 = (f32[2,32,16]{1,2,0:T(8,128)S(1)}, f32[2,32,16]{1,2,0:T(8,128)}, u32[]{:S(2)}) copy-start(f32[2,32,16]{1,2,0:T(8,128)} %param.15) | copy-start | bytes 12292
Sparse Core Ops, SparseCore 0:
  236.8 146.8 all-reduce.3
Sparse Core Ops, SparseCore 1:
  239.2 77.3 all-gather.1
  408.4 72.2 reduce-scatter.3
where the time goes:
time: 500 us; the launch traced here: 490 us
  waiting for transfers between devices  222 us (44%)
  local copies, waits for them, and re-layouts  166 us (33%)
  other arithmetic  45.8 us (9%)
  matrix products  30.9 us (6%)
  between operations  16 us (3%)
  starting transfers between devices  8.95 us (2%)
    psum x1, waiting for transfers between devices, shards(): summed = lax.psum(stacked, ('replica', 'tm'))  146 us
    slice x54, local copies, waits for them, and re-layouts, tap_patches(): padded[:, along_time:along_time + 2 * out_frames:2, along_rows:along_rows...  120 us
    unnamed x4, waiting for transfers between devices  72.9 us
    scatter-add x27, other arithmetic, spread_back(): total = total.at[:, along_time:along_time + 2 * out_frames:2, along_rows:...  40.8 us
    unnamed x58, local copies, waits for them, and re-layouts  33.9 us
    dot_general x1, matrix products, shards(): tap_mixed = jnp.einsum('lst,ltij->lsij', tap_mix, summed, precision=highest)  10.7 us
    dot_general x1, matrix products, shards(): jnp.einsum('lik,lskj->lsij', lax.all_gather(left_panels, 'fsdp', axis=1,...  10.1 us
  transfers between devices with their start and end apart: 6, of which 4 were waited for; matrix products, arithmetic and copies ran while one was open for 12% of the time, Pallas kernels for 0%

commit v1 on v0

v1 whole, which is shorter than its diff:
```python
import functools

import jax
import jax.numpy as jnp
from jax import lax
from jax.experimental import pallas as pl
from jax.experimental.pallas import tpu as pltpu
from jax.sharding import PartitionSpec as P

TAPS = 27
MESH = pl.DeviceIdType.MESH
F32 = jnp.float32
BF16 = jnp.bfloat16
NZ = 16
NX = 4
NY = 4
COLS = 896


def dot(a, b):
    return lax.dot_general(a, b, (((1,), (0,)), ((), ())), preferred_element_type=F32)


def dot_t(a, b):
    return lax.dot_general(a, b, (((1,), (1,)), ((), ())), preferred_element_type=F32)


def split(v):
    high = v.astype(BF16)
    return high, (v - high.astype(F32)).astype(BF16)


def gather_rows(b, c, rows, wide):
    shape = (64, wide * wide)
    position = lax.broadcasted_iota(jnp.int32, shape, 0)
    cell = lax.broadcasted_iota(jnp.int32, shape, 1)
    yh, xh = position >> 3, position & 7
    if rows == "read":
        hit = cell == (2 * yh + (b - 1)) * wide + 2 * xh + (c - 1)
        if c == 0:
            hit = hit & (xh > 0)
    else:
        yq, xq = cell >> 2, cell & 3
        hit = (yh == 2 * yq + (b - 1)) & (xh == 2 * xq + (c - 1))
    return jnp.where(hit, 1.0, 0.0).astype(BF16)


def kernel(
    x_ref, k1_ref, k2_ref, og_ref, mix_ref, left_ref, right_ref, out_ref,
    patches, spread, og_own, og_in, halo_out, halo_in, lhalo_out, lhalo_in,
    acts, rtiles, rall, xl, mixed32, mixed, mixpad,
    u_send, u_in, u_own, s1_send, s1_in, s2, s2_send, s2_in,
    og_sem, halo_sem, lhalo_sem, act_ssem, act_rsem, rz_ssem, rz_rsem,
    rp_ssem, rp_rsem, rc_sem, uc_ssem, uc_rsem, p1_ssem, p1_rsem, p2_ssem, p2_rsem,
):
    z = lax.axis_index("fsdp")
    rep = lax.axis_index("replica")
    tm = lax.axis_index("tm")
    core = rep % 2
    y = (rep // 2) % NY
    x_lo = rep // (2 * NY)
    xi = tm * 2 + x_lo
    chip = xi * NY + y

    def at(xi_to, y_to, core_to):
        return {"replica": ((xi_to % 2) * NY + y_to) * 2 + core_to, "tm": xi_to // 2}

    def chip_at(d):
        to = (chip + d) % (NX * NY)
        return at(to // NY, to % NY, core)

    def remote(src, dst, ssem, rsem, device):
        return pltpu.make_async_remote_copy(
            src_ref=src, dst_ref=dst, send_sem=ssem, recv_sem=rsem,
            device_id=device, device_id_type=MESH,
        )

    other_core = {"replica": rep + 1 - 2 * core}
    other_half = {"tm": 1 - tm}

    barrier = pltpu.get_barrier_semaphore()

    def greet_z(d, carry):
        pl.semaphore_signal(barrier, inc=1, device_id={"fsdp": (z + d) % NZ}, device_id_type=MESH)
        return carry

    def greet_plane(d, carry):
        pl.semaphore_signal(barrier, inc=1, device_id=chip_at(d), device_id_type=MESH)
        return carry

    lax.fori_loop(1, NZ, greet_z, 0)
    lax.fori_loop(1, NX * NY, greet_plane, 0)
    pl.semaphore_signal(barrier, inc=1, device_id=other_core, device_id_type=MESH)

    select = jnp.concatenate([gather_rows(t // 3, t % 3, "read", 16) for t in range(9)], axis=0)
    for slot, frame in enumerate((0, 2, 1, 3)):
        picked = dot(select, x_ref[frame]).astype(BF16)
        for t in range(9):
            patches[t, slot * 64 : (slot + 1) * 64, :] = picked[t * 64 : (t + 1) * 64]

    lane = lax.broadcasted_iota(jnp.int32, (32, 128), 1)
    first_half = lane < 64
    left0 = split(left_ref[0])
    left1 = split(left_ref[1])
    acc = jnp.zeros((96, 256), F32)
    for t in range(9):
        stack = jnp.concatenate(
            [k1_ref[t], k1_ref[9 + t], k1_ref[18 + t], left0[0], left0[1]], axis=0
        )
        res = dot_t(stack, patches[t])
        acc = acc + res[:96]
        lx = res[96:128] + res[128:160]
        xl[0, 9 + t] = lx[:, :128]
        xl[0, 18 + t] = lx[:, 128:]
        turned = pltpu.roll(lx[:, 128:], 64, 1)
        xl[0, t] = turned
        lhalo_out[t] = turned.astype(BF16)
    turned_pre = pltpu.roll(acc[:32, 128:], 64, 1)
    halo_out[...] = turned_pre

    row = lax.broadcasted_iota(jnp.int32, (32, 128), 0)
    tile = dot(right_ref[0].astype(BF16), jnp.where(lane == row, 1.0, 0.0).astype(BF16))
    tile = tile + dot(right_ref[1].astype(BF16), jnp.where(lane == row + 32, 1.0, 0.0).astype(BF16))
    rtiles[pl.ds(z, 1)] = tile.astype(BF16)[None]

    pl.semaphore_wait(barrier, NZ - 1 + NX * NY - 1 + 1)

    halo = remote(halo_out, halo_in, halo_sem.at[0], halo_sem.at[1], other_half)
    halo.start()
    og_copy = remote(og_ref, og_in, og_sem.at[0], og_sem.at[1], other_half)
    og_copy.start()

    def rz(d, block):
        return remote(
            rtiles.at[z], rtiles.at[block], rz_ssem.at[d - 1], rz_rsem.at[d - 1],
            {"fsdp": (z + d) % NZ},
        )

    def rz_start(d, carry):
        rz(d, z).start()
        return carry

    lax.fori_loop(1, NZ, rz_start, 0)
    lhalo = remote(lhalo_out, lhalo_in, lhalo_sem.at[0], lhalo_sem.at[1], other_half)
    lhalo.start()

    place = jnp.concatenate([gather_rows(t // 3, t % 3, "spread", 4) for t in range(9)], axis=0)
    for r in range(4):
        og_own[0, 4 * r : 4 * r + 4, :] = og_ref[r].astype(F32)
    picked = dot(place, og_own[0].astype(BF16)).astype(BF16)
    for t in range(9):
        spread[t, :64, :] = picked[t * 64 : (t + 1) * 64]
    og_copy.wait_recv()
    keep_next = jnp.where(tm == 0, 1.0, 0.0).astype(F32)
    for r in range(4):
        og_own[1, 4 * r : 4 * r + 4, :] = og_in[r].astype(F32) * keep_next
    picked = dot(place, og_own[1].astype(BF16)).astype(BF16)
    for t in range(9):
        spread[t, 64:, :] = picked[t * 64 : (t + 1) * 64]
    back = jnp.zeros((96, 128), F32)
    for t in range(9):
        stack = jnp.concatenate(
            [k2_ref[t], k2_ref[9 + t], k2_ref[18 + t], left1[0], left1[1]], axis=0
        )
        res = dot_t(stack, spread[t])
        back = back + res[:96]
        lo = res[96:128] + res[128:160]
        xl[1, t] = jnp.where(first_half, 0.0, lo)
        xl[1, 9 + t] = jnp.where(first_half, lo, 0.0)
        xl[1, 18 + t] = jnp.where(first_half, 0.0, pltpu.roll(lo, 64, 1))
    hidden_grad = jnp.where(first_half, back[32:64], pltpu.roll(back[64:96], 64, 1) + back[:32])

    halo.wait_recv()
    keep_prior = jnp.where(tm == 1, 1.0, 0.0).astype(F32)
    pre = acc[32:64, :128] + acc[64:96, 128:]
    pre = pre + jnp.where(first_half, halo_in[...] * keep_prior, turned_pre)
    sig = jax.nn.sigmoid(pre)
    hidden = pre * sig
    pre_grad = hidden_grad * sig * (1.0 + pre * (1.0 - sig))
    acts[pl.ds(z, 1)] = jnp.concatenate([hidden, pre_grad], axis=0).astype(BF16)[None]

    def act(d, block):
        return remote(
            acts.at[z], acts.at[block], act_ssem.at[d - 1], act_rsem.at[d - 1],
            {"fsdp": (z + d) % NZ},
        )

    def act_start(d, carry):
        act(d, z).start()
        return carry

    lax.fori_loop(1, NZ, act_start, 0)

    def rz_wait(d, carry):
        rz(d, (z - d) % NZ).wait_recv()
        return carry

    lax.fori_loop(1, NZ, rz_wait, 0)
    mine = core * NX * NY + chip
    lane16 = lax.broadcasted_iota(jnp.int32, (16, 128), 1) >> 5
    for g in range(4):
        four = [rtiles[4 * g + v].astype(F32) for v in range(4)]
        for layer in range(2):
            piece = jnp.zeros((16, 128), F32)
            for v in range(4):
                shift = (32 * (v - layer)) % 128
                moved = pltpu.roll(four[v], shift, 1) if shift else four[v]
                piece = jnp.where(lane16 == v, moved, piece)
            rall[pl.ds(mine, 1), layer, :, g * 128 : (g + 1) * 128] = piece.astype(BF16)[None]

    def rp(d, block):
        return remote(
            rall.at[mine], rall.at[block], rp_ssem.at[d - 1], rp_rsem.at[d - 1], chip_at(d)
        )

    def rp_start(d, carry):
        rp(d, mine).start()
        return carry

    lax.fori_loop(1, NX * NY, rp_start, 0)

    lhalo.wait_recv()
    for t in range(9):
        xl[0, t] = jnp.where(first_half, lhalo_in[t].astype(F32) * keep_prior, xl[0, t])
    for t in range(27, 32):
        for layer in range(2):
            xl[layer, t] = jnp.zeros((32, 128), F32)
    big_row = lax.broadcasted_iota(jnp.int32, (256, 256), 0)
    big_col = lax.broadcasted_iota(jnp.int32, (256, 256), 1)
    same = (big_row & 7) == (big_col & 7)
    er = lax.broadcasted_iota(jnp.int32, (256, 32), 0)
    ec = lax.broadcasted_iota(jnp.int32, (256, 32), 1)
    expand = jnp.where((er >> 3) == ec, 1.0, 0.0).astype(BF16)
    mixpad[...] = jnp.zeros((2, 32, 32), F32)
    for layer in range(2):
        mixpad[layer, 0:27, 0:27] = mix_ref[layer]
        wide = []
        for part in split(mixpad[layer]):
            tall = dot(expand, part).astype(BF16)
            wide.append(jnp.where(same, dot_t(tall, expand), 0.0).astype(BF16))
        block = jnp.concatenate(
            [xl[layer, :, 8 * q : 8 * q + 8, :].reshape(256, 128) for q in range(4)], axis=1
        )
        high, low = split(block)
        res = dot(wide[0], high) + dot(wide[0], low) + dot(wide[1], high)
        for q in range(4):
            mixed32[:, 8 * q : 8 * q + 8, :] = res[:, 128 * q : 128 * q + 128].reshape(32, 8, 128)
        mixed[layer] = mixed32[0:28].reshape(COLS, 128).astype(BF16)

    def rp_wait(d, carry):
        rp(d, core * NX * NY + (chip - d) % (NX * NY)).wait_recv()
        return carry

    lax.fori_loop(1, NX * NY, rp_wait, 0)
    half = pl.ds(core * NX * NY, NX * NY)
    far_half = pl.ds((1 - core) * NX * NY, NX * NY)
    rc = remote(rall.at[half], rall.at[half], rc_sem.at[0], rc_sem.at[1], other_core)
    rc.start()

    def act_wait(d, carry):
        act(d, (z - d) % NZ).wait_recv()
        return carry

    lax.fori_loop(1, NZ, act_wait, 0)
    own_acts = [acts[:, 32:64, :].reshape(512, 128), acts[:, 0:32, :].reshape(512, 128)]

    def partial(panel_rows, layer):
        turned_act = dot(rall[panel_rows, layer].reshape(256, 512), own_acts[layer])
        high, low = split(turned_act)
        return dot_t(high, mixed[layer]) + dot_t(low, mixed[layer])

    remote(rall.at[far_half], rall.at[far_half], rc_sem.at[0], rc_sem.at[1], other_core).wait_recv()
    uc = []
    for layer in (1, 0):
        res = partial(far_half, layer).astype(BF16)
        for a in range(4):
            for b in range(4):
                spot = (a, b) if layer == 0 else (b, a)
                u_send[(layer, *spot)] = res[(a * 4 + b) * 16 : (a * 4 + b + 1) * 16]
        copy = remote(u_send.at[layer], u_in.at[layer], uc_ssem.at[layer], uc_rsem.at[layer], other_core)
        copy.start()
        uc.append((layer, copy))
    for layer in (1, 0):
        res = partial(half, layer)
        for a in range(4):
            for b in range(4):
                spot = (a, b) if layer == 0 else (b, a)
                u_own[(layer, *spot)] = res[(a * 4 + b) * 16 : (a * 4 + b + 1) * 16]

    first = {0: xi, 1: y}
    second = {0: y, 1: xi}

    def first_to(layer, f):
        return at(f, y, core) if layer == 0 else at(xi, f, core)

    def second_to(layer, f):
        return at(xi, f, core) if layer == 0 else at(f, y, core)

    p1 = {}
    for layer, copy in uc:
        copy.wait_recv()
        for d in range(1, 4):
            f = (first[layer] + d) % 4
            total = u_own[layer, pl.ds(f, 1)] + u_in[layer, pl.ds(f, 1)].astype(F32)
            s1_send[layer, d - 1] = total[0].astype(BF16)
            p1[layer, d] = remote(
                s1_send.at[layer, d - 1], s1_in.at[layer, d - 1],
                p1_ssem.at[layer, d - 1], p1_rsem.at[layer, d - 1], first_to(layer, f),
            )
            p1[layer, d].start()
    p2 = {}
    for layer in (1, 0):
        f = first[layer]
        total = (u_own[layer, pl.ds(f, 1)] + u_in[layer, pl.ds(f, 1)].astype(F32))[0]
        for d in range(1, 4):
            p1[layer, d].wait_recv()
            total = total + s1_in[layer, d - 1].astype(F32)
        s2[layer] = total
        for d in range(1, 4):
            g = (second[layer] + d) % 4
            s2_send[layer, d - 1] = s2[layer, pl.ds(g, 1)][0].astype(BF16)
            p2[layer, d] = remote(
                s2_send.at[layer, d - 1], s2_in.at[layer, d - 1],
                p2_ssem.at[layer, d - 1], p2_rsem.at[layer, d - 1], second_to(layer, g),
            )
            p2[layer, d].start()
    for layer in (1, 0):
        total = s2[layer, pl.ds(second[layer], 1)][0]
        for d in range(1, 4):
            p2[layer, d].wait_recv()
            total = total + s2_in[layer, d - 1].astype(F32)
        for s in range(TAPS):
            out_ref[layer, s] = total[:, 32 * s : 32 * s + 32].astype(BF16)

    halo.wait_send()
    og_copy.wait_send()
    lhalo.wait_send()
    rc.wait_send()

    def z_sent(d, carry):
        rz(d, z).wait_send()
        act(d, z).wait_send()
        rp(d, mine).wait_send()
        return carry

    lax.fori_loop(1, NZ, z_sent, 0)
    for layer, copy in uc:
        copy.wait_send()
        for d in range(1, 4):
            p1[layer, d].wait_send()
            p2[layer, d].wait_send()


def shards(clip_input, first_kernel, second_kernel, out_grad, tap_mix, left_panels, right_panels):
    vmem = functools.partial(pltpu.VMEM)
    dma = pltpu.SemaphoreType.DMA
    operands = (
        clip_input.reshape(4, 256, 512),
        first_kernel.swapaxes(1, 2),
        second_kernel,
        out_grad.reshape(4, 4, 512),
        tap_mix,
        left_panels,
        right_panels.swapaxes(1, 2),
    )
    spec = pl.BlockSpec(memory_space=pltpu.VMEM)
    out = pl.pallas_call(
        kernel,
        name="shampoo_update",
        out_shape=jax.ShapeDtypeStruct((2, TAPS, 16, 32), BF16),
        in_specs=[spec] * len(operands),
        out_specs=spec,
        scratch_shapes=[
            vmem((9, 256, 512), BF16),
            vmem((9, 128, 512), BF16),
            vmem((2, 16, 512), F32),
            vmem((4, 4, 512), BF16),
            vmem((32, 128), F32),
            vmem((32, 128), F32),
            vmem((9, 32, 128), BF16),
            vmem((9, 32, 128), BF16),
            vmem((NZ, 64, 128), BF16),
            vmem((NZ, 16, 128), BF16),
            vmem((2 * NX * NY, 2, 16, 512), BF16),
            vmem((2, 32, 32, 128), F32),
            vmem((32, 32, 128), F32),
            vmem((2, COLS, 128), BF16),
            vmem((2, 32, 32), F32),
            vmem((2, 4, 4, 16, COLS), BF16),
            vmem((2, 4, 4, 16, COLS), BF16),
            vmem((2, 4, 4, 16, COLS), F32),
            vmem((2, 3, 4, 16, COLS), BF16),
            vmem((2, 3, 4, 16, COLS), BF16),
            vmem((2, 4, 16, COLS), F32),
            vmem((2, 3, 16, COLS), BF16),
            vmem((2, 3, 16, COLS), BF16),
            dma((2,)), dma((2,)), dma((2,)),
            dma((NZ - 1,)), dma((NZ - 1,)), dma((NZ - 1,)), dma((NZ - 1,)),
            dma((NX * NY - 1,)), dma((NX * NY - 1,)),
            dma((2,)), dma((2,)), dma((2,)),
            dma((2, 3)), dma((2, 3)), dma((2, 3)), dma((2, 3)),
        ],
        compiler_params=pltpu.CompilerParams(collective_id=0, has_side_effects=True),
    )(*operands)
    return out.swapaxes(2, 3)


def solution(mesh):
    in_specs = (
        P("replica", "tm", None, None, None),
        P(None, None, "fsdp"),
        P(None, "fsdp", None),
        P("replica", "tm", None, None, None),
        P(),
        P(None, "fsdp", None),
        P(None, "fsdp", ("replica", "tm")),
    )
    out_specs = P(None, None, "fsdp", ("replica", "tm"))
    return jax.shard_map(shards, mesh=mesh, in_specs=in_specs, out_specs=out_specs, check_vma=False)
```

time: 500 us -> 56.7 us (0.11)
  the two profiles are of different devices: /device:TPU:6 before, /device:TPU:1 now
where the time goes in v1:
time: 56.7 us; the launch traced here: 56.5 us
  Pallas kernels  53.5 us (94%)
  local copies, waits for them, and re-layouts  3 us (5%)
    pallas_call x1, Pallas kernels, shards(): pl.pallas_call(kernel, name='shampoo_update', out_shape=jax.ShapeDtypeStr...  53.5 us
    unnamed x2, local copies, waits for them, and re-layouts  3 us

profile of v1, /device:TPU:1, one launch (start us, length us, event | category | flops | bytes accessed | tf_op | source)
XLA Modules:
  0.0 56.5 jit_solution(10816838686250975959)
XLA Ops:
  0.0 1.4 %copy.8.mix_ref = f32[2,27,27]{2,1,0:T(8,128)} copy(f32[2,27,27]{2,0,1:T(2,128)} %param.11) | data formatting | bytes 11664 | tf_op args[4]
  1.4 53.5 %shampoo_update.1 = bf16[2,27,16,32]{3,2,1,0:T(8,128)(2,1)} custom-call(bf16[4,256,512]{2,1,0:T(8,128)(2,1)} %bitcast.5, bf16[27,32,512]{2,1,0:T(8,128)(2,1)} %bitcast.7, bf16[27,32,512]{2,1,0:T(8,128)(2,1)} %k2_ref.1, bf16[4,4,512]{2,1,0:T(4,128)(2,1)} %bitcast.8, f32[2,27,27]{2,1,0:T(8,128)} %copy.8.mix_ref, f32[2,32,512]{2,1,0:T(8,128)} %left_ref.1, ...), custom_call_target="tpu_custom_call" | custom-call | tf_op jit(solution)/shard_map/shampoo_update/pallas_call | solution.py:367
  54.8 1.6 %copy.10 = bf16[2,27,32,16]{2,3,1,0:T(8,128)(2,1)} copy(bf16[2,27,32,16]{2,3,1,0:T(8,128)(2,1)} %bitcast.6) | data formatting | bytes 110592

commit v2 on v1

v2 whole, which is shorter than its diff:
```python
import jax
import jax.numpy as jnp
from jax import lax
from jax.experimental import pallas as pl
from jax.experimental.pallas import tpu as pltpu
from jax.sharding import PartitionSpec as P

TAPS = 27
MESH = pl.DeviceIdType.MESH
F32 = jnp.float32
BF16 = jnp.bfloat16
NZ = 16
NX = 4
NY = 4
COLS = 896


def dot(a, b):
    return lax.dot_general(a, b, (((1,), (0,)), ((), ())), preferred_element_type=F32)


def dot_t(a, b):
    return lax.dot_general(a, b, (((1,), (1,)), ((), ())), preferred_element_type=F32)


def split(v):
    high = v.astype(BF16)
    return high, (v - high.astype(F32)).astype(BF16)


def gather_rows(b, c, rows, wide):
    shape = (64, wide * wide)
    position = lax.broadcasted_iota(jnp.int32, shape, 0)
    cell = lax.broadcasted_iota(jnp.int32, shape, 1)
    yh, xh = position >> 3, position & 7
    if rows == "read":
        hit = cell == (2 * yh + (b - 1)) * wide + 2 * xh + (c - 1)
        if c == 0:
            hit = hit & (xh > 0)
    else:
        yq, xq = cell >> 2, cell & 3
        hit = (yh == 2 * yq + (b - 1)) & (xh == 2 * xq + (c - 1))
    return jnp.where(hit, 1.0, 0.0).astype(BF16)


def kernel(
    x_hbm, k1_hbm, k2_hbm, og_hbm, mix_hbm, left_hbm, right_hbm, out_ref,
    x_ref, k1_ref, k2_ref, og_ref, mix_ref, left_ref, right_ref,
    patches, spread, og_wide, halo_out, halo_in, lhalo_out, lhalo_in,
    acts, acts_far, rtiles, rall, xl, mixed32, mixed, mixed_far, mixpad,
    u, p1_send, p1_in, s2, s2_send, s2_in,
    in_sem, halo_sem, lhalo_sem, act_ssem, act_rsem, rz_ssem, rz_rsem,
    rp_ssem, rp_rsem, cf_ssem, cf_rsem, mc_ssem, mc_rsem, p1_ssem, p1_rsem, p2_ssem, p2_rsem,
):
    z = lax.axis_index("fsdp")
    rep = lax.axis_index("replica")
    tm = lax.axis_index("tm")
    core = rep % 2
    y = (rep // 2) % NY
    x_lo = rep // (2 * NY)
    xi = tm * 2 + x_lo
    chip = xi * NY + y

    def at(xi_to, y_to):
        return {"replica": ((xi_to % 2) * NY + y_to) * 2 + core, "tm": xi_to // 2}

    def chip_at(d):
        to = (chip + d) % (NX * NY)
        return at(to // NY, to % NY)

    def remote(src, dst, ssem, rsem, device):
        return pltpu.make_async_remote_copy(
            src_ref=src, dst_ref=dst, send_sem=ssem, recv_sem=rsem,
            device_id=device, device_id_type=MESH,
        )

    other_core = {"replica": rep + 1 - 2 * core}
    other_half = {"tm": 1 - tm}

    fetch = [
        pltpu.make_async_copy(src, dst, in_sem.at[n])
        for n, (src, dst) in enumerate(
            [(x_hbm.at[f], x_ref.at[f]) for f in range(4)]
            + [
                (right_hbm, right_ref), (left_hbm, left_ref), (k1_hbm, k1_ref),
                (og_hbm, og_ref), (k2_hbm, k2_ref), (mix_hbm, mix_ref),
            ]
        )
    ]
    for copy in fetch:
        copy.start()

    barrier = pltpu.get_barrier_semaphore()

    def greet(device):
        pl.semaphore_signal(barrier, inc=1, device_id=device, device_id_type=MESH)

    for d in (4, 12, 3, 13, 2, 14, 1, 15):
        greet({"fsdp": (z + d) % NZ})

    def greet_plane(d, carry):
        greet(chip_at(d))
        return carry

    lax.fori_loop(1, NX * NY, greet_plane, 0)
    greet(other_core)

    lane = lax.broadcasted_iota(jnp.int32, (32, 128), 1)
    first_half = lane < 64
    is_first = jnp.where(tm == 0, 1.0, 0.0).astype(F32)
    is_last = 1.0 - is_first

    fetch[4].wait()
    row = lax.broadcasted_iota(jnp.int32, (32, 128), 0)
    tile = dot(right_ref[0].astype(BF16), jnp.where(lane == row, 1.0, 0.0).astype(BF16))
    tile = tile + dot(right_ref[1].astype(BF16), jnp.where(lane == row + 32, 1.0, 0.0).astype(BF16))
    rtiles[pl.ds(z, 1)] = tile.astype(BF16)[None]

    select = jnp.concatenate([gather_rows(t // 3, t % 3, "read", 16) for t in range(9)], axis=0)
    for slot, frame in enumerate((0, 2, 1, 3)):
        fetch[frame].wait()
        picked = dot(select, x_ref[frame]).astype(BF16)
        for t in range(9):
            patches[t, slot * 64 : (slot + 1) * 64, :] = picked[t * 64 : (t + 1) * 64]

    fetch[5].wait()
    left0 = split(left_ref[0])
    left1 = split(left_ref[1])
    fetch[6].wait()
    acc = jnp.zeros((96, 256), F32)
    for t in range(9):
        stack = jnp.concatenate(
            [k1_ref[t], k1_ref[9 + t], k1_ref[18 + t], left0[0], left0[1]], axis=0
        )
        res = dot_t(stack, patches[t])
        acc = acc + res[:96]
        lx = res[96:128] + res[128:160]
        xl[0, 9 + t] = lx[:, :128]
        xl[0, 18 + t] = lx[:, 128:]
        xl[0, t] = pltpu.roll(lx[:, 128:], 64, 1)
    turned_pre = pltpu.roll(acc[:32, 128:], 64, 1)

    pl.semaphore_wait(barrier, 8 + NX * NY - 1 + 1)

    class Ring:
        def __init__(self, buf, ssem, rsem):
            self.buf, self.ssem, self.rsem = buf, ssem, rsem

        def copy(self, block, d, device):
            return remote(
                self.buf.at[block], self.buf.at[block],
                self.ssem.at[d - 1], self.rsem.at[d - 1], {"fsdp": device},
            )

        def start(self):
            for e in (4, 3, 2, 1):
                self.copy(z, e, (z + e) % NZ).start()
                self.copy(z, NZ - e, (z + NZ - e) % NZ).start()

        def wait(self, d):
            self.copy((z + NZ - d) % NZ, d, (z + d) % NZ).wait_recv()

        def forward(self):
            self.wait(4)
            for k in (4, 3, 2, 1):
                self.copy((z + NZ - 4) % NZ, 4 + k, (z + k) % NZ).start()
            self.wait(12)
            for k in (3, 2, 1):
                self.copy((z + 4) % NZ, 12 - k, (z + NZ - k) % NZ).start()

        def sent(self):
            for d in range(1, NZ):
                self.copy(z, d, (z + d) % NZ).wait_send()

    rz = Ring(rtiles, rz_ssem, rz_rsem)
    act = Ring(acts, act_ssem, act_rsem)
    rz.start()

    place = jnp.concatenate([gather_rows(t // 3, t % 3, "spread", 4) for t in range(9)], axis=0)
    fetch[7].wait()
    for r in range(4):
        og_wide[4 * r : 4 * r + 4, :] = og_ref[r].astype(F32)
    picked = dot(place, og_wide[...].astype(BF16)).astype(BF16)
    for t in range(9):
        spread[t, :64, :] = picked[t * 64 : (t + 1) * 64]
        spread[t, 64:, :] = picked[t * 64 : (t + 1) * 64]
    fetch[8].wait()
    back = jnp.zeros((96, 128), F32)
    for t in range(9):
        stack = jnp.concatenate(
            [k2_ref[t], k2_ref[9 + t], k2_ref[18 + t], left1[0], left1[1]], axis=0
        )
        res = dot_t(stack, spread[t])
        back = back + res[:96]
        lo = res[96:128] + res[128:160]
        xl[1, 9 + t] = jnp.where(first_half, lo, 0.0)
        xl[1, 18 + t] = jnp.where(first_half, 0.0, lo)
        lhalo_out[t] = (xl[0, t] * is_first + lo * is_last).astype(BF16)
    halo_out[...] = turned_pre * is_first + back[:32] * is_last
    halo = remote(halo_out, halo_in, halo_sem.at[0], halo_sem.at[1], other_half)
    halo.start()

    fetch[9].wait()
    big_row = lax.broadcasted_iota(jnp.int32, (256, 256), 0)
    big_col = lax.broadcasted_iota(jnp.int32, (256, 256), 1)
    same = (big_row & 7) == (big_col & 7)
    er = lax.broadcasted_iota(jnp.int32, (256, 32), 0)
    ec = lax.broadcasted_iota(jnp.int32, (256, 32), 1)
    expand = jnp.where((er >> 3) == ec, 1.0, 0.0).astype(BF16)
    mixpad[...] = jnp.zeros((2, 32, 32), F32)
    wide = []
    for layer in range(2):
        mixpad[layer, 0:27, 0:27] = mix_ref[:, layer, :]
        for part in split(mixpad[layer]):
            tall = dot(expand, part).astype(BF16)
            wide.append(jnp.where(same, dot_t(tall, expand), 0.0).astype(BF16))

    halo.wait_recv()
    received = halo_in[...]
    pre = acc[32:64, :128] + acc[64:96, 128:]
    pre = pre + jnp.where(first_half, received * is_last, turned_pre)
    hidden_grad = jnp.where(first_half, back[32:64], back[64:96] + received * is_first)
    sig = jax.nn.sigmoid(pre)
    hidden = pre * sig
    pre_grad = hidden_grad * sig * (1.0 + pre * (1.0 - sig))
    acts[pl.ds(z, 1)] = jnp.concatenate([hidden, pre_grad], axis=0).astype(BF16)[None]
    act.start()

    def share(d):
        block = (z + NZ - d) % NZ
        return remote(acts.at[block], acts_far.at[block], cf_ssem.at[d], cf_rsem.at[d], other_core)

    share(0).start()
    lhalo = remote(lhalo_out, lhalo_in, lhalo_sem.at[0], lhalo_sem.at[1], other_half)
    lhalo.start()

    rz.forward()
    act.forward()

    for d in (1, 15, 2, 14, 3, 13, 5, 11, 6, 10, 7, 9, 8):
        rz.wait(d)
    lane16 = lax.broadcasted_iota(jnp.int32, (16, 128), 1) >> 5
    for g in range(4):
        four = [rtiles[4 * g + v].astype(F32) for v in range(4)]
        for layer in range(2):
            piece = jnp.zeros((16, 128), F32)
            for v in range(4):
                shift = (32 * (v - layer)) % 128
                moved = pltpu.roll(four[v], shift, 1) if shift else four[v]
                piece = jnp.where(lane16 == v, moved, piece)
            rall[layer, pl.ds(chip, 1), :, g * 128 : (g + 1) * 128] = piece.astype(BF16)[None]

    def rp(layer, d, block):
        return remote(
            rall.at[layer, block], rall.at[layer, block],
            rp_ssem.at[layer, d - 1], rp_rsem.at[layer, d - 1], chip_at(d),
        )

    for layer in (1, 0):

        def rp_start(d, carry, layer=layer):
            rp(layer, d, chip).start()
            return carry

        lax.fori_loop(1, NX * NY, rp_start, 0)

    lhalo.wait_recv()
    for t in range(9):
        got = lhalo_in[t].astype(F32)
        xl[0, t] = jnp.where(first_half, got * is_last, xl[0, t])
        xl[1, t] = jnp.where(first_half, 0.0, got * is_first)
    mc = {}
    for layer in (1, 0):
        for t in range(27, 32):
            xl[layer, t] = jnp.zeros((32, 128), F32)
        block = jnp.concatenate(
            [xl[layer, :, 8 * q : 8 * q + 8, :].reshape(256, 128) for q in range(4)], axis=1
        )
        high, low = split(block)
        res = dot(wide[2 * layer], high) + dot(wide[2 * layer], low) + dot(wide[2 * layer + 1], high)
        for q in range(4):
            mixed32[:, 8 * q : 8 * q + 8, :] = res[:, 128 * q : 128 * q + 128].reshape(32, 8, 128)
        mixed[layer] = mixed32[0:28].reshape(COLS, 128).astype(BF16)
        mc[layer] = remote(
            mixed.at[layer], mixed_far.at[layer], mc_ssem.at[layer], mc_rsem.at[layer], other_core
        )
        mc[layer].start()

    for d in (4, 12):
        share(d).start()
    for d in (1, 15, 2, 14, 3, 13, 5, 11, 6, 10, 7, 9, 8):
        act.wait(d)
        share(d).start()
    for d in range(NZ):
        share(d).wait_recv()

    first = {0: xi, 1: y}
    second = {0: y, 1: xi}

    def first_to(layer, f):
        return at(f, y) if layer == 0 else at(xi, f)

    def second_to(layer, f):
        return at(xi, f) if layer == 0 else at(f, y)

    lower, upper = pl.ds(0, 2), pl.ds(2, 2)

    def send1(layer, n, step):
        return remote(
            p1_send.at[layer, n], p1_in.at[layer, n], p1_ssem.at[layer, n], p1_rsem.at[layer, n],
            first_to(layer, (first[layer] + step) % 4),
        )

    for layer in (1, 0):

        def rp_wait(d, carry, layer=layer):
            rp(layer, d, (chip + NX * NY - d) % (NX * NY)).wait_recv()
            return carry

        lax.fori_loop(1, NX * NY, rp_wait, 0)
        mc[layer].wait_recv()
        rows = pl.ds(0, 32) if layer == 1 else pl.ds(32, 32)
        both = jnp.concatenate(
            [acts[:, rows, :].reshape(512, 128), acts_far[:, rows, :].reshape(512, 128)], axis=1
        )
        turned_act = dot(rall[layer].reshape(256, 512), both)
        high, low = split(turned_act)
        mix = jnp.concatenate([mixed[layer], mixed_far[layer]], axis=1)
        res = dot_t(high, mix) + dot_t(low, mix)
        for a in range(4):
            for b in range(4):
                spot = (a, b) if layer == 0 else (b, a)
                u[(layer, *spot)] = res[(a * 4 + b) * 16 : (a * 4 + b + 1) * 16]
        f = first[layer]
        for n, off, part, step in (
            (0, 2, lower, 1), (1, 2, upper, 3), (2, 1, upper, 1), (3, 3, lower, 3),
        ):
            p1_send[layer, n] = u[layer, pl.ds((f + off) % 4, 1), part][0].astype(BF16)
            send1(layer, n, step).start()

    for layer in (1, 0):
        f = first[layer]
        for n, source, off, part, step in ((4, 0, 1, lower, 1), (5, 1, 3, upper, 3)):
            send1(layer, source, step).wait_recv()
            total = u[layer, pl.ds((f + off) % 4, 1), part][0] + p1_in[layer, source].astype(F32)
            p1_send[layer, n] = total.astype(BF16)
            send1(layer, n, step).start()
    p2 = {}
    for layer in (1, 0):
        f = first[layer]
        for direct, passed, part in ((3, 4, lower), (2, 5, upper)):
            send1(layer, direct, 1).wait_recv()
            send1(layer, passed, 1).wait_recv()
            total = u[layer, pl.ds(f, 1), part][0]
            total = total + p1_in[layer, direct].astype(F32) + p1_in[layer, passed].astype(F32)
            s2[layer, part] = total
        for d in range(1, 4):
            g = (second[layer] + d) % 4
            s2_send[layer, d - 1] = s2[layer, pl.ds(g, 1)][0].astype(BF16)
            p2[layer, d] = remote(
                s2_send.at[layer, d - 1], s2_in.at[layer, d - 1],
                p2_ssem.at[layer, d - 1], p2_rsem.at[layer, d - 1], second_to(layer, g),
            )
            p2[layer, d].start()
    for layer in (1, 0):
        total = s2[layer, pl.ds(second[layer], 1)][0]
        for d in range(1, 4):
            p2[layer, d].wait_recv()
            total = total + s2_in[layer, d - 1].astype(F32)
        for s in range(TAPS):
            out_ref[layer, s] = total[:, 32 * s : 32 * s + 32].astype(BF16)

    halo.wait_send()
    lhalo.wait_send()
    rz.sent()
    act.sent()
    for d in range(NZ):
        share(d).wait_send()
    for layer in (1, 0):

        def rp_sent(d, carry, layer=layer):
            rp(layer, d, chip).wait_send()
            return carry

        lax.fori_loop(1, NX * NY, rp_sent, 0)
        mc[layer].wait_send()
        for n in range(6):
            send1(layer, n, 1).wait_send()
        for d in range(1, 4):
            p2[layer, d].wait_send()


def shards(clip_input, first_kernel, second_kernel, out_grad, tap_mix, left_panels, right_panels):
    vmem = pltpu.VMEM
    dma = pltpu.SemaphoreType.DMA
    operands = (
        clip_input.reshape(4, 256, 512),
        first_kernel.swapaxes(1, 2),
        second_kernel,
        out_grad.reshape(4, 4, 512),
        tap_mix.swapaxes(0, 1),
        left_panels,
        right_panels.swapaxes(1, 2),
    )
    out = pl.pallas_call(
        kernel,
        name="shampoo_update",
        out_shape=jax.ShapeDtypeStruct((2, TAPS, 16, 32), BF16),
        in_specs=[pl.BlockSpec(memory_space=pl.ANY)] * len(operands),
        out_specs=pl.BlockSpec(memory_space=pltpu.VMEM),
        scratch_shapes=[
            *(vmem(v.shape, v.dtype) for v in operands),
            vmem((9, 256, 512), BF16),
            vmem((9, 128, 512), BF16),
            vmem((16, 512), F32),
            vmem((32, 128), F32),
            vmem((32, 128), F32),
            vmem((9, 32, 128), BF16),
            vmem((9, 32, 128), BF16),
            vmem((NZ, 64, 128), BF16),
            vmem((NZ, 64, 128), BF16),
            vmem((NZ, 16, 128), BF16),
            vmem((2, NX * NY, 16, 512), BF16),
            vmem((2, 32, 32, 128), F32),
            vmem((32, 32, 128), F32),
            vmem((2, COLS, 128), BF16),
            vmem((2, COLS, 128), BF16),
            vmem((2, 32, 32), F32),
            vmem((2, 4, 4, 16, COLS), F32),
            vmem((2, 6, 2, 16, COLS), BF16),
            vmem((2, 6, 2, 16, COLS), BF16),
            vmem((2, 4, 16, COLS), F32),
            vmem((2, 3, 16, COLS), BF16),
            vmem((2, 3, 16, COLS), BF16),
            dma((10,)), dma((2,)), dma((2,)),
            dma((NZ - 1,)), dma((NZ - 1,)), dma((NZ - 1,)), dma((NZ - 1,)),
            dma((2, NX * NY - 1)), dma((2, NX * NY - 1)),
            dma((NZ,)), dma((NZ,)), dma((2,)), dma((2,)),
            dma((2, 6)), dma((2, 6)), dma((2, 3)), dma((2, 3)),
        ],
        compiler_params=pltpu.CompilerParams(collective_id=0, has_side_effects=True),
    )(*operands)
    return out.swapaxes(2, 3)


def solution(mesh):
    in_specs = (
        P("replica", "tm", None, None, None),
        P(None, None, "fsdp"),
        P(None, "fsdp", None),
        P("replica", "tm", None, None, None),
        P(),
        P(None, "fsdp", None),
        P(None, "fsdp", ("replica", "tm")),
    )
    out_specs = P(None, None, "fsdp", ("replica", "tm"))
    return jax.shard_map(shards, mesh=mesh, in_specs=in_specs, out_specs=out_specs, check_vma=False)
```

time: 56.7 us -> 50.7 us (0.89)
  the two profiles are of different devices: /device:TPU:1 before, /device:TPU:2 now
where the time goes in v2:
time: 50.7 us; the launch traced here: 50.5 us
  Pallas kernels  48.9 us (96%)
  local copies, waits for them, and re-layouts  1.64 us (3%)
    pallas_call x1, Pallas kernels, shards(): pl.pallas_call(kernel, name='shampoo_update', out_shape=jax.ShapeDtypeStr...  48.9 us
    unnamed x1, local copies, waits for them, and re-layouts  1.64 us

profile of v2, /device:TPU:2, one launch (start us, length us, event | category | flops | bytes accessed | tf_op | source)
XLA Modules:
  0.0 50.5 jit_solution(15662735654650533659)
XLA Ops:
  0.0 48.9 %shampoo_update.1 = bf16[2,27,16,32]{3,2,1,0:T(8,128)(2,1)} custom-call(bf16[4,256,512]{2,1,0:T(8,128)(2,1)} %bitcast.6, bf16[27,32,512]{2,1,0:T(8,128)(2,1)} %bitcast.7, bf16[27,32,512]{2,1,0:T(8,128)(2,1)} %k2_hbm.1, bf16[4,4,512]{2,1,0:T(4,128)(2,1)} %bitcast.10, f32[27,2,27]{2,1,0:T(2,128)} %bitcast.9, f32[2,32,512]{2,1,0:T(8,128)} %left_hbm.1, ...), custom_call_target="tpu_custom_call" | custom-call | tf_op jit(solution)/shard_map/shampoo_update/pallas_call | solution.py:405
  48.9 1.6 %copy.9 = bf16[2,27,32,16]{2,3,1,0:T(8,128)(2,1)} copy(bf16[2,27,32,16]{2,3,1,0:T(8,128)(2,1)} %bitcast.8) | data formatting | bytes 110592

commit v3 on v2

v3 whole, which is shorter than its diff:
```python
import jax
import jax.numpy as jnp
from jax import lax
from jax.experimental import pallas as pl
from jax.experimental.pallas import tpu as pltpu
from jax.sharding import PartitionSpec as P

TAPS = 27
MESH = pl.DeviceIdType.MESH
F32 = jnp.float32
BF16 = jnp.bfloat16
NZ = 16
NX = 4
NY = 4
COLS = 896


def rem(a, n):
    return lax.rem(a, jnp.int32(n))


def div(a, n):
    return lax.div(a, jnp.int32(n))


def dot(a, b):
    return lax.dot_general(a, b, (((1,), (0,)), ((), ())), preferred_element_type=F32)


def dot_t(a, b):
    return lax.dot_general(a, b, (((1,), (1,)), ((), ())), preferred_element_type=F32)


def split(v):
    high = v.astype(BF16)
    return high, (v - high.astype(F32)).astype(BF16)


def gather_rows(b, c, rows, wide):
    shape = (64, wide * wide)
    position = lax.broadcasted_iota(jnp.int32, shape, 0)
    cell = lax.broadcasted_iota(jnp.int32, shape, 1)
    yh, xh = position >> 3, position & 7
    if rows == "read":
        hit = cell == (2 * yh + (b - 1)) * wide + 2 * xh + (c - 1)
        if c == 0:
            hit = hit & (xh > 0)
    else:
        yq, xq = cell >> 2, cell & 3
        hit = (yh == 2 * yq + (b - 1)) & (xh == 2 * xq + (c - 1))
    return jnp.where(hit, 1.0, 0.0).astype(BF16)


def kernel(
    x_hbm, k1_hbm, k2_hbm, og_hbm, mix_hbm, left_hbm, right_hbm, out_ref,
    x_ref, k1_ref, k2_ref, og_ref, mix_ref, left_ref, right_ref,
    patches, spread, og_wide, halo_out, halo_in, lhalo_out, lhalo_in,
    acts, acts_far, rtiles, rall, xl, mixed32, mixed, mixed_far, mixpad,
    u, p1_send, p1_in, s2_send, s2_in,
    in_sem, halo_sem, lhalo_sem, act_ssem, act_rsem, rz_ssem, rz_rsem,
    rp_sem, cf_sem, mc_sem, p1_ssem, p1_rsem, p2_sem,
):
    z = lax.axis_index("fsdp")
    rep = lax.axis_index("replica")
    tm = lax.axis_index("tm")
    core = rem(rep, 2)
    y = rem(div(rep, 2), NY)
    x_lo = div(rep, 2 * NY)
    xi = tm * 2 + x_lo
    chip = xi * NY + y

    x_at = [rem(xi + d, NX) for d in range(NX)]
    x_part = [(rem(v, 2) * 2 * NY, div(v, 2)) for v in x_at]
    y_part = [rem(y + d, NY) * 2 + core for d in range(NY)]
    plane = [(dx, dy) for dx in (2, 1, 3, 0) for dy in (2, 1, 3, 0) if dx or dy]

    def at(dx, dy):
        return {"replica": x_part[dx][0] + y_part[dy], "tm": x_part[dx][1]}

    def up(d):
        return rem(z + d, NZ)

    def remote(src, dst, ssem, rsem, device):
        return pltpu.make_async_remote_copy(
            src_ref=src, dst_ref=dst, send_sem=ssem, recv_sem=rsem,
            device_id=device, device_id_type=MESH,
        )

    other_core = {"replica": rep + 1 - 2 * core}
    other_half = {"tm": 1 - tm}

    fetch = [
        pltpu.make_async_copy(src, dst, in_sem.at[n])
        for n, (src, dst) in enumerate(
            [(x_hbm.at[f], x_ref.at[f]) for f in range(4)]
            + [
                (right_hbm, right_ref), (left_hbm, left_ref), (k1_hbm, k1_ref),
                (og_hbm, og_ref), (k2_hbm, k2_ref), (mix_hbm, mix_ref),
            ]
        )
    ]
    for n in (1, 3, 6, 7, 8, 4, 0, 2, 5, 9):
        fetch[n].start()

    barrier = pltpu.get_barrier_semaphore()

    def greet(device):
        pl.semaphore_signal(barrier, inc=1, device_id=device, device_id_type=MESH)

    for d in (4, 12, 3, 13, 2, 14, 1, 15):
        greet({"fsdp": up(d)})

    for dx, dy in plane:
        greet(at(dx, dy))
    greet(other_core)

    lane = lax.broadcasted_iota(jnp.int32, (32, 128), 1)
    first_half = lane < 64
    is_first = jnp.where(tm == 0, 1.0, 0.0).astype(F32)
    is_last = 1.0 - is_first

    select = jnp.concatenate([gather_rows(t // 3, t % 3, "read", 16) for t in range(9)], axis=0)

    def pick(pair, frames):
        for slot, frame in enumerate(frames):
            fetch[frame].wait()
            picked = dot(select, x_ref[frame]).astype(BF16)
            for t in range(9):
                patches[pair, t, slot * 64 : (slot + 1) * 64, :] = picked[t * 64 : (t + 1) * 64]

    pick(1, (1, 3))
    fetch[6].wait()
    odd = jnp.zeros((64, 128), F32)
    for t in range(9):
        odd = odd + dot_t(jnp.concatenate([k1_ref[t], k1_ref[18 + t]], axis=0), patches[1, t])
    turned_pre = pltpu.roll(odd[:32], 64, 1)

    fetch[4].wait()
    row = lax.broadcasted_iota(jnp.int32, (32, 128), 0)
    tile = dot(right_ref[0].astype(BF16), jnp.where(lane == row, 1.0, 0.0).astype(BF16))
    tile = tile + dot(right_ref[1].astype(BF16), jnp.where(lane == row + 32, 1.0, 0.0).astype(BF16))
    rtiles[pl.ds(z, 1)] = tile.astype(BF16)[None]

    class Ring:
        def __init__(self, buf, ssem, rsem, group):
            self.buf, self.ssem, self.rsem, self.group = buf, ssem, rsem, group

        def copy(self, back, d):
            block = up(NZ - back)
            gap = (back + d) % NZ
            kind = {4: 0, 12: 1}.get(gap)
            kind = self.group(block, gap) if kind is None else kind
            return remote(
                self.buf.at[block], self.buf.at[block], self.ssem.at[0], self.rsem.at[kind],
                {"fsdp": up(d)},
            )

        def start(self):
            for e in (4, 3, 2, 1):
                self.copy(0, e).start()
                self.copy(0, NZ - e).start()

        def arrived(self, count, kind):
            part = self.buf.at[pl.ds(0, count)]
            remote(part, part, self.ssem.at[0], self.rsem.at[kind], {"fsdp": up(1)}).wait_recv()

        def forward(self):
            self.arrived(1, 0)
            for k in (4, 3, 2, 1):
                self.copy(4, k).start()
            self.arrived(1, 1)
            for k in (3, 2, 1):
                self.copy(12, NZ - k).start()

        def sent(self):
            part = self.buf.at[pl.ds(0, NZ - 1)]
            remote(part, part, self.ssem.at[0], self.rsem.at[0], {"fsdp": up(1)}).wait_send()

    rz = Ring(rtiles, rz_ssem, rz_rsem, lambda block, gap: 2 + div(block, 4))
    act = Ring(acts, act_ssem, act_rsem, lambda block, gap: gap - 2 if 4 < gap < 12 else 2)
    place = jnp.concatenate([gather_rows(t // 3, t % 3, "spread", 4) for t in range(9)], axis=0)
    fetch[7].wait()
    for r in range(4):
        og_wide[4 * r : 4 * r + 4, :] = og_ref[r].astype(F32)
    picked = dot(place, og_wide[...].astype(BF16)).astype(BF16)
    for t in range(9):
        spread[t, :64, :] = picked[t * 64 : (t + 1) * 64]
        spread[t, 64:, :] = picked[t * 64 : (t + 1) * 64]
    fetch[8].wait()
    back = jnp.zeros((96, 128), F32)
    for t in range(9):
        stack = jnp.concatenate([k2_ref[t], k2_ref[9 + t], k2_ref[18 + t]], axis=0)
        back = back + dot_t(stack, spread[t])
    halo_out[...] = turned_pre * is_first + back[:32] * is_last

    pl.semaphore_wait(barrier, 8 + NX * NY - 1 + 1)

    halo = remote(halo_out, halo_in, halo_sem.at[0], halo_sem.at[1], other_half)
    halo.start()
    rz.start()

    pick(0, (0, 2))
    even = jnp.zeros((32, 128), F32)
    for t in range(9):
        even = even + dot_t(k1_ref[9 + t], patches[0, t])

    rz.forward()

    halo.wait_recv()
    received = halo_in[...]
    pre = even + odd[32:] + jnp.where(first_half, received * is_last, turned_pre)
    hidden_grad = jnp.where(first_half, back[32:64], back[64:96] + received * is_first)
    sig = jax.nn.sigmoid(pre)
    hidden = pre * sig
    pre_grad = hidden_grad * sig * (1.0 + pre * (1.0 - sig))
    acts[pl.ds(z, 1)] = jnp.concatenate([hidden, pre_grad], axis=0).astype(BF16)[None]
    act.start()

    def share(d):
        block = up(NZ - d)
        return remote(acts.at[block], acts_far.at[block], cf_sem.at[0], cf_sem.at[1], other_core)

    share(0).start()

    fetch[5].wait()
    left0 = jnp.concatenate(split(left_ref[0]), axis=0)
    left1 = jnp.concatenate(split(left_ref[1]), axis=0)
    for t in range(9):
        res = dot_t(left0, patches[1, t])
        lx = res[:32] + res[32:]
        turned = pltpu.roll(lx, 64, 1)
        xl[0, 18 + t] = lx
        xl[0, t] = turned
        res = dot_t(left1, spread[t])
        lo = res[:32] + res[32:]
        xl[1, 9 + t] = jnp.where(first_half, lo, 0.0)
        xl[1, 18 + t] = jnp.where(first_half, 0.0, lo)
        lhalo_out[t] = (turned * is_first + lo * is_last).astype(BF16)
    lhalo = remote(lhalo_out, lhalo_in, lhalo_sem.at[0], lhalo_sem.at[1], other_half)
    lhalo.start()
    own_group = div(z, 4)
    lane16 = lax.broadcasted_iota(jnp.int32, (16, 128), 1) >> 5

    def spread_panels(g):
        opposite = own_group == (g + 2) % 4

        @pl.when(opposite)
        def _():
            rz.arrived(4, 2 + g)

        @pl.when(jnp.logical_not(opposite))
        def _():
            rz.arrived(3, 2 + g)

        four = [rtiles[4 * g + v].astype(F32) for v in range(4)]
        for layer in range(2):
            piece = jnp.zeros((16, 128), F32)
            for v in range(4):
                shift = (32 * (v - layer)) % 128
                moved = pltpu.roll(four[v], shift, 1) if shift else four[v]
                piece = jnp.where(lane16 == v, moved, piece)
            rall[g, layer, pl.ds(chip, 1)] = piece.astype(BF16)[None]
        for layer in (1, 0):
            for dx, dy in plane:
                part = rall.at[g, layer, chip]
                kind = 2 + layer if g == 2 else 1
                remote(part, part, rp_sem.at[0], rp_sem.at[kind], at(dx, dy)).start()

    for g in (0, 1, 3):
        spread_panels(g)
    act.forward()
    spread_panels(2)
    for d in (4, 12):
        share(d).start()
    act.arrived(6, 2)
    for d in (1, 15, 2, 14, 3, 13):
        share(d).start()

    for t in range(9):
        res = dot_t(left0, patches[0, t])
        xl[0, 9 + t] = res[:32] + res[32:]

    fetch[9].wait()
    big_row = lax.broadcasted_iota(jnp.int32, (256, 256), 0)
    big_col = lax.broadcasted_iota(jnp.int32, (256, 256), 1)
    same = (big_row & 7) == (big_col & 7)
    er = lax.broadcasted_iota(jnp.int32, (256, 32), 0)
    ec = lax.broadcasted_iota(jnp.int32, (256, 32), 1)
    expand = jnp.where((er >> 3) == ec, 1.0, 0.0).astype(BF16)
    mixpad[...] = jnp.zeros((2, 32, 32), F32)
    wide = []
    for layer in range(2):
        mixpad[layer, 0:27, 0:27] = mix_ref[:, layer, :]
        for part in split(mixpad[layer]):
            tall = dot(expand, part).astype(BF16)
            wide.append(jnp.where(same, dot_t(tall, expand), 0.0).astype(BF16))

    lhalo.wait_recv()
    for t in range(9):
        edge = lhalo_in[t].astype(F32)
        xl[0, t] = jnp.where(first_half, edge * is_last, xl[0, t])
        xl[1, t] = jnp.where(first_half, 0.0, edge * is_first)
    mc = {}
    for layer in (1, 0):
        for t in range(27, 32):
            xl[layer, t] = jnp.zeros((32, 128), F32)
        block = jnp.concatenate(
            [xl[layer, :, 8 * q : 8 * q + 8, :].reshape(256, 128) for q in range(4)], axis=1
        )
        high, low = split(block)
        res = dot(wide[2 * layer], high) + dot(wide[2 * layer], low) + dot(wide[2 * layer + 1], high)
        for q in range(4):
            mixed32[:, 8 * q : 8 * q + 8, :] = res[:, 128 * q : 128 * q + 128].reshape(32, 8, 128)
        mixed[layer] = mixed32[0:28].reshape(COLS, 128).astype(BF16)
        mc[layer] = remote(
            mixed.at[layer], mixed_far.at[layer], mc_sem.at[2], mc_sem.at[layer], other_core
        )
        mc[layer].start()

    for d in (5, 11, 6, 10, 7, 9, 8):
        act.arrived(1, d - 2)
        share(d).start()
    everything = remote(acts, acts_far, cf_sem.at[0], cf_sem.at[1], other_core)
    everything.wait_recv()

    first = {0: xi, 1: y}
    second = {0: y, 1: xi}
    offs = (2, 1, 3, 0)

    def along(layer, step):
        return at(step, 0) if layer == 0 else at(0, step)

    def across(layer, step):
        return at(0, step) if layer == 0 else at(step, 0)

    def columns(k, n):
        cut = 512 if k < 2 else 384
        return slice(0, cut) if n in (0, 3, 4) else slice(cut, COLS)

    def send1(layer, k, n):
        step = 1 if n in (0, 2, 4) else 3
        cols = columns(k, n)
        width = slice(0, cols.stop - cols.start)
        return remote(
            p1_send.at[layer, k, n, :, width], p1_in.at[layer, k, n, :, width],
            p1_ssem.at[0], p1_rsem.at[layer, k, 0 if n < 2 else 1], along(layer, step),
        )

    def arrived1(layer, k, late):
        rows = s2_in.at[0, pl.ds(0, 1 + late)]
        remote(rows, rows, p1_ssem.at[0], p1_rsem.at[layer, k, late], along(layer, 1)).wait_recv()

    def partial(layer, k, off, cols):
        f, g = rem(first[layer] + off, 4), rem(second[layer] + offs[k], 4)
        return u[layer, pl.ds(f, 1), pl.ds(g, 1), :, cols][0, 0]

    def got(layer, k, n):
        cols = columns(k, n)
        return p1_in[layer, k, n, :, : cols.stop - cols.start].astype(F32)

    def put(layer, k, n, value):
        cols = columns(k, n)
        p1_send[layer, k, n, :, : cols.stop - cols.start] = value.astype(BF16)
        send1(layer, k, n).start()

    def panels(part, kind):
        return remote(part, part, rp_sem.at[0], rp_sem.at[kind], at(1, 0))

    some = pl.ds(0, NX * NY - 1)
    panels(rall.at[pl.ds(0, 3), :, some], 1).wait_recv()
    for layer in (1, 0):
        mc[layer].wait_recv()
        panels(rall.at[2, layer, some], 2 + layer).wait_recv()
        rows = pl.ds(0, 32) if layer == 1 else pl.ds(32, 32)
        both = jnp.concatenate(
            [acts[:, rows, :].reshape(512, 128), acts_far[:, rows, :].reshape(512, 128)], axis=1
        )
        panel = jnp.concatenate([rall[g, layer].reshape(256, 128) for g in range(4)], axis=1)
        turned_act = dot(panel, both)
        high, low = split(turned_act)
        mix = jnp.concatenate([mixed[layer], mixed_far[layer]], axis=1)
        res = dot_t(high, mix) + dot_t(low, mix)
        for a in range(4):
            for b in range(4):
                spot = (a, b) if layer == 0 else (b, a)
                u[(layer, *spot)] = res[(a * 4 + b) * 16 : (a * 4 + b + 1) * 16]
        for k in range(4):
            for n in (0, 1):
                put(layer, k, n, partial(layer, k, 2, columns(k, n)))
        for k in range(4):
            put(layer, k, 2, partial(layer, k, 1, columns(k, 2)))
            put(layer, k, 3, partial(layer, k, 3, columns(k, 3)))

    halo.wait_send()
    lhalo.wait_send()
    rz.sent()
    act.sent()
    everything.wait_send()
    panels(rall.at[:, :, some], 1).wait_send()
    remote(mixed, mixed_far, mc_sem.at[2], mc_sem.at[0], other_core).wait_send()

    for k in range(4):
        for layer in (1, 0):
            arrived1(layer, k, 0)
            put(layer, k, 4, partial(layer, k, 1, columns(k, 4)) + got(layer, k, 0))
            put(layer, k, 5, partial(layer, k, 3, columns(k, 5)) + got(layer, k, 1))
    kept = {}
    for k in range(4):
        for layer in (1, 0):
            arrived1(layer, k, 1)
            left = partial(layer, k, 0, columns(k, 4)) + got(layer, k, 3) + got(layer, k, 4)
            right = partial(layer, k, 0, columns(k, 5)) + got(layer, k, 2) + got(layer, k, 5)
            total = jnp.concatenate([left, right], axis=1)
            d = offs[k]
            if d == 0:
                kept[layer] = total
                continue
            s2_send[layer, d - 1] = total.astype(BF16)
            remote(
                s2_send.at[layer, d - 1], s2_in.at[layer, d - 1],
                p2_sem.at[2], p2_sem.at[layer], across(layer, d),
            ).start()
    for layer in (1, 0):
        total = kept[layer]
        remote(
            s2_send.at[layer], s2_in.at[layer], p2_sem.at[2], p2_sem.at[layer], across(layer, 1)
        ).wait_recv()
        for d in (1, 3, 2):
            total = total + s2_in[layer, d - 1].astype(F32)
        for s in range(TAPS):
            out_ref[layer, s] = total[:, 32 * s : 32 * s + 32].astype(BF16)

    rows = u.at[0, pl.ds(0, 3)]
    remote(rows, rows, p1_ssem.at[0], p1_rsem.at[0, 0, 0], along(0, 1)).wait_send()
    remote(s2_send, s2_in, p2_sem.at[2], p2_sem.at[0], across(0, 1)).wait_send()


def shards(clip_input, first_kernel, second_kernel, out_grad, tap_mix, left_panels, right_panels):
    vmem = pltpu.VMEM
    dma = pltpu.SemaphoreType.DMA
    operands = (
        clip_input.reshape(4, 256, 512),
        first_kernel.swapaxes(1, 2),
        second_kernel,
        out_grad.reshape(4, 4, 512),
        tap_mix.swapaxes(0, 1),
        left_panels,
        right_panels.swapaxes(1, 2),
    )
    out = pl.pallas_call(
        kernel,
        name="shampoo_update",
        out_shape=jax.ShapeDtypeStruct((2, TAPS, 16, 32), BF16),
        in_specs=[pl.BlockSpec(memory_space=pl.ANY)] * len(operands),
        out_specs=pl.BlockSpec(memory_space=pltpu.VMEM),
        scratch_shapes=[
            *(vmem(v.shape, v.dtype) for v in operands),
            vmem((2, 9, 128, 512), BF16),
            vmem((9, 128, 512), BF16),
            vmem((16, 512), F32),
            vmem((32, 128), F32),
            vmem((32, 128), F32),
            vmem((9, 32, 128), BF16),
            vmem((9, 32, 128), BF16),
            vmem((NZ, 64, 128), BF16),
            vmem((NZ, 64, 128), BF16),
            vmem((NZ, 16, 128), BF16),
            vmem((4, 2, NX * NY, 16, 128), BF16),
            vmem((2, 32, 32, 128), F32),
            vmem((32, 32, 128), F32),
            vmem((2, COLS, 128), BF16),
            vmem((2, COLS, 128), BF16),
            vmem((2, 32, 32), F32),
            vmem((2, 4, 4, 16, COLS), F32),
            vmem((2, 4, 6, 16, 512), BF16),
            vmem((2, 4, 6, 16, 512), BF16),
            vmem((2, 3, 16, COLS), BF16),
            vmem((2, 3, 16, COLS), BF16),
            dma((10,)), dma((2,)), dma((2,)),
            dma((1,)), dma((10,)), dma((1,)), dma((6,)),
            dma((4,)), dma((2,)), dma((3,)), dma((1,)), dma((2, 4, 2)), dma((3,)),
        ],
        compiler_params=pltpu.CompilerParams(collective_id=0, has_side_effects=True),
    )(*operands)
    return out.swapaxes(2, 3)


def solution(mesh):
    in_specs = (
        P("replica", "tm", None, None, None),
        P(None, None, "fsdp"),
        P(None, "fsdp", None),
        P("replica", "tm", None, None, None),
        P(),
        P(None, "fsdp", None),
        P(None, "fsdp", ("replica", "tm")),
    )
    out_specs = P(None, None, "fsdp", ("replica", "tm"))
    return jax.shard_map(shards, mesh=mesh, in_specs=in_specs, out_specs=out_specs, check_vma=False)
```

time: 50.7 us -> 45.4 us (0.90)
  the two profiles are of different devices: /device:TPU:2 before, /device:TPU:1 now
where the time goes in v3:
time: 45.4 us; the launch traced here: 45.2 us
  Pallas kernels  43.6 us (96%)
  local copies, waits for them, and re-layouts  1.64 us (4%)
    pallas_call x1, Pallas kernels, shards(): pl.pallas_call(kernel, name='shampoo_update', out_shape=jax.ShapeDtypeStr...  43.6 us
    unnamed x1, local copies, waits for them, and re-layouts  1.64 us

profile of v3, /device:TPU:1, one launch (start us, length us, event | category | flops | bytes accessed | tf_op | source)
XLA Modules:
  0.0 45.2 jit_solution(14685876703715153367)
XLA Ops:
  0.0 43.6 %shampoo_update.1 = bf16[2,27,16,32]{3,2,1,0:T(8,128)(2,1)} custom-call(bf16[4,256,512]{2,1,0:T(8,128)(2,1)} %bitcast.6, bf16[27,32,512]{2,1,0:T(8,128)(2,1)} %bitcast.7, bf16[27,32,512]{2,1,0:T(8,128)(2,1)} %k2_hbm.1, bf16[4,4,512]{2,1,0:T(4,128)(2,1)} %bitcast.10, f32[27,2,27]{2,1,0:T(2,128)} %bitcast.9, f32[2,32,512]{2,1,0:T(8,128)} %left_hbm.1, ...), custom_call_target="tpu_custom_call" | custom-call | tf_op jit(solution)/shard_map/shampoo_update/pallas_call | solution.py:450
  43.6 1.6 %copy.9 = bf16[2,27,32,16]{2,3,1,0:T(8,128)(2,1)} copy(bf16[2,27,32,16]{2,3,1,0:T(8,128)(2,1)} %bitcast.8) | data formatting | bytes 110592

commit v4 on v3

--- a/solution.py
+++ b/solution.py
@@ -99,7 +99,7 @@
             ]
         )
     ]
-    for n in (1, 3, 6, 7, 8, 4, 0, 2, 5, 9):
+    for n in (1, 3, 6):
         fetch[n].start()
 
     barrier = pltpu.get_barrier_semaphore()
@@ -113,6 +113,8 @@
     for dx, dy in plane:
         greet(at(dx, dy))
     greet(other_core)
+    for n in (7, 8, 4, 0, 2, 5, 9):
+        fetch[n].start()
 
     lane = lax.broadcasted_iota(jnp.int32, (32, 128), 1)
     first_half = lane < 64
@@ -139,7 +141,10 @@
     row = lax.broadcasted_iota(jnp.int32, (32, 128), 0)
     tile = dot(right_ref[0].astype(BF16), jnp.where(lane == row, 1.0, 0.0).astype(BF16))
     tile = tile + dot(right_ref[1].astype(BF16), jnp.where(lane == row + 32, 1.0, 0.0).astype(BF16))
+    tile = tile[:8] + pltpu.roll(tile[8:], 64, 1)
     rtiles[pl.ds(z, 1)] = tile.astype(BF16)[None]
+
+    even_z = rem(z, 2) == 0
 
     class Ring:
         def __init__(self, buf, ssem, rsem, group):
@@ -166,9 +171,19 @@
 
         def forward(self):
             self.arrived(1, 0)
-            for k in (4, 3, 2, 1):
+
+            @pl.when(even_z)
+            def _():
+                self.copy(4, 4).start()
+
+            for k in (3, 2, 1):
                 self.copy(4, k).start()
             self.arrived(1, 1)
+
+            @pl.when(jnp.logical_not(even_z))
+            def _():
+                self.copy(12, NZ - 4).start()
+
             for k in (3, 2, 1):
                 self.copy(12, NZ - k).start()
 
@@ -253,6 +268,7 @@
             rz.arrived(3, 2 + g)
 
         four = [rtiles[4 * g + v].astype(F32) for v in range(4)]
+        four = [jnp.concatenate([v, pltpu.roll(v, 64, 1)], axis=0) for v in four]
         for layer in range(2):
             piece = jnp.zeros((16, 128), F32)
             for v in range(4):
@@ -368,6 +384,23 @@
 
     some = pl.ds(0, NX * NY - 1)
     panels(rall.at[pl.ds(0, 3), :, some], 1).wait_recv()
+    operands = {}
+
+    def product(layer, offsets):
+        both, mix = operands[layer]
+        spots = [rem(first[layer] + off, 4) for off in offsets]
+        rows = []
+        for f in spots:
+            for b in range(4):
+                to = f * 4 + b if layer == 0 else b * 4 + f
+                rows.append(
+                    jnp.concatenate([rall[g, layer, pl.ds(to, 1)][0] for g in range(4)], axis=1)
+                )
+        high, low = split(dot(jnp.concatenate(rows, axis=0), both))
+        res = dot_t(high, mix) + dot_t(low, mix)
+        for n, f in enumerate(spots):
+            u[layer, pl.ds(f, 1)] = res[64 * n : 64 * n + 64].reshape(1, 4, 16, COLS)
+
     for layer in (1, 0):
         mc[layer].wait_recv()
         panels(rall.at[2, layer, some], 2 + layer).wait_recv()
@@ -375,18 +408,13 @@
         both = jnp.concatenate(
             [acts[:, rows, :].reshape(512, 128), acts_far[:, rows, :].reshape(512, 128)], axis=1
         )
-        panel = jnp.concatenate([rall[g, layer].reshape(256, 128) for g in range(4)], axis=1)
-        turned_act = dot(panel, both)
-        high, low = split(turned_act)
-        mix = jnp.concatenate([mixed[layer], mixed_far[layer]], axis=1)
-        res = dot_t(high, mix) + dot_t(low, mix)
-        for a in range(4):
-            for b in range(4):
-                spot = (a, b) if layer == 0 else (b, a)
-                u[(layer, *spot)] = res[(a * 4 + b) * 16 : (a * 4 + b + 1) * 16]
+        operands[layer] = both, jnp.concatenate([mixed[layer], mixed_far[layer]], axis=1)
+        product(layer, (2,))
         for k in range(4):
             for n in (0, 1):
                 put(layer, k, n, partial(layer, k, 2, columns(k, n)))
+    for layer in (1, 0):
+        product(layer, (1, 3, 0))
         for k in range(4):
             put(layer, k, 2, partial(layer, k, 1, columns(k, 2)))
             put(layer, k, 3, partial(layer, k, 3, columns(k, 3)))
@@ -464,7 +492,7 @@
             vmem((9, 32, 128), BF16),
             vmem((NZ, 64, 128), BF16),
             vmem((NZ, 64, 128), BF16),
-            vmem((NZ, 16, 128), BF16),
+            vmem((NZ, 8, 128), BF16),
             vmem((4, 2, NX * NY, 16, 128), BF16),
             vmem((2, 32, 32, 128), F32),
             vmem((32, 32, 128), F32),

time: 45.4 us -> 44 us (0.969)
  Pallas kernels: 43.6 us -> 42.2 us
    pallas_call x1, Pallas kernels: 43.6 us -> 42.2 us  [shards(): pl.pallas_call(kernel, name='shampoo_update', out_shape=jax.ShapeDtypeStr...]
where the time goes in v4:
time: 44 us; the launch traced here: 43.8 us
  Pallas kernels  42.2 us (96%)
  local copies, waits for them, and re-layouts  1.64 us (4%)
    pallas_call x1, Pallas kernels, shards(): pl.pallas_call(kernel, name='shampoo_update', out_shape=jax.ShapeDtypeStr...  42.2 us
    unnamed x1, local copies, waits for them, and re-layouts  1.64 us

profile of v4, /device:TPU:1, one launch (start us, length us, event | category | flops | bytes accessed | tf_op | source)
XLA Modules:
  0.0 43.8 jit_solution(11929984939477854014)
XLA Ops:
  0.0 42.2 %shampoo_update.1 = bf16[2,27,16,32]{3,2,1,0:T(8,128)(2,1)} custom-call(bf16[4,256,512]{2,1,0:T(8,128)(2,1)} %bitcast.6, bf16[27,32,512]{2,1,0:T(8,128)(2,1)} %bitcast.7, bf16[27,32,512]{2,1,0:T(8,128)(2,1)} %k2_hbm.1, bf16[4,4,512]{2,1,0:T(4,128)(2,1)} %bitcast.10, f32[27,2,27]{2,1,0:T(2,128)} %bitcast.9, f32[2,32,512]{2,1,0:T(8,128)} %left_hbm.1, ...), custom_call_target="tpu_custom_call" | custom-call | tf_op jit(solution)/shard_map/shampoo_update/pallas_call | solution.py:478
  42.2 1.6 %copy.9 = bf16[2,27,32,16]{2,3,1,0:T(8,128)(2,1)} copy(bf16[2,27,32,16]{2,3,1,0:T(8,128)(2,1)} %bitcast.8) | data formatting | bytes 110592

commit v5 on v4

--- a/solution.py
+++ b/solution.py
@@ -99,7 +99,7 @@
             ]
         )
     ]
-    for n in (1, 3, 6):
+    for n in (7, 1, 3, 6):
         fetch[n].start()
 
     barrier = pltpu.get_barrier_semaphore()
@@ -113,7 +113,7 @@
     for dx, dy in plane:
         greet(at(dx, dy))
     greet(other_core)
-    for n in (7, 8, 4, 0, 2, 5, 9):
+    for n in (8, 4, 0, 2, 5, 9):
         fetch[n].start()
 
     lane = lax.broadcasted_iota(jnp.int32, (32, 128), 1)
@@ -122,6 +122,15 @@
     is_last = 1.0 - is_first
 
     select = jnp.concatenate([gather_rows(t // 3, t % 3, "read", 16) for t in range(9)], axis=0)
+
+    place = jnp.concatenate([gather_rows(t // 3, t % 3, "spread", 4) for t in range(9)], axis=0)
+    fetch[7].wait()
+    for r in range(4):
+        og_wide[4 * r : 4 * r + 4, :] = og_ref[r].astype(F32)
+    picked = dot(place, og_wide[...].astype(BF16)).astype(BF16)
+    for t in range(9):
+        spread[t, :64, :] = picked[t * 64 : (t + 1) * 64]
+        spread[t, 64:, :] = picked[t * 64 : (t + 1) * 64]
 
     def pick(pair, frames):
         for slot, frame in enumerate(frames):
@@ -193,14 +202,6 @@
 
     rz = Ring(rtiles, rz_ssem, rz_rsem, lambda block, gap: 2 + div(block, 4))
     act = Ring(acts, act_ssem, act_rsem, lambda block, gap: gap - 2 if 4 < gap < 12 else 2)
-    place = jnp.concatenate([gather_rows(t // 3, t % 3, "spread", 4) for t in range(9)], axis=0)
-    fetch[7].wait()
-    for r in range(4):
-        og_wide[4 * r : 4 * r + 4, :] = og_ref[r].astype(F32)
-    picked = dot(place, og_wide[...].astype(BF16)).astype(BF16)
-    for t in range(9):
-        spread[t, :64, :] = picked[t * 64 : (t + 1) * 64]
-        spread[t, 64:, :] = picked[t * 64 : (t + 1) * 64]
     fetch[8].wait()
     back = jnp.zeros((96, 128), F32)
     for t in range(9):

time: 44 us -> 43.8 us (level)
  no operation moved by 1% of the time
where the time goes in v5:
time: 43.8 us; the launch traced here: 43.6 us
  Pallas kernels  42 us (96%)
  local copies, waits for them, and re-layouts  1.64 us (4%)
    pallas_call x1, Pallas kernels, shards(): pl.pallas_call(kernel, name='shampoo_update', out_shape=jax.ShapeDtypeStr...  42 us
    unnamed x1, local copies, waits for them, and re-layouts  1.64 us

profile of v5, /device:TPU:1, one launch (start us, length us, event | category | flops | bytes accessed | tf_op | source)
XLA Modules:
  0.0 43.6 jit_solution(5697122712318836166)
XLA Ops:
  0.0 42.0 %shampoo_update.1 = bf16[2,27,16,32]{3,2,1,0:T(8,128)(2,1)} custom-call(bf16[4,256,512]{2,1,0:T(8,128)(2,1)} %bitcast.6, bf16[27,32,512]{2,1,0:T(8,128)(2,1)} %bitcast.7, bf16[27,32,512]{2,1,0:T(8,128)(2,1)} %k2_hbm.1, bf16[4,4,512]{2,1,0:T(4,128)(2,1)} %bitcast.10, f32[27,2,27]{2,1,0:T(2,128)} %bitcast.9, f32[2,32,512]{2,1,0:T(8,128)} %left_hbm.1, ...), custom_call_target="tpu_custom_call" | custom-call | tf_op jit(solution)/shard_map/shampoo_update/pallas_call | solution.py:479
  42.0 1.6 %copy.9 = bf16[2,27,32,16]{2,3,1,0:T(8,128)(2,1)} copy(bf16[2,27,32,16]{2,3,1,0:T(8,128)(2,1)} %bitcast.8) | data formatting | bytes 110592
